TPU v7x, 1024 devices: a whole 4x8x16 slice. The times are simulated.
1024 devices in a mesh: dp: 64 (over z_lo, y, core), rep: 16 (over z_hi, x).
Axes of the slice: x: 4, y: 8, z: 16 (z_hi: 4, z_lo: 4; z = z_hi * 4 + z_lo), core: 2. Of those that a mesh axis runs over, the one named last changes fastest.
Arguments:
- clips: bfloat16 [1024, 1024, 256], P(('dp', 'rep')), may hold values from -6 to 6
- cotangent: bfloat16 [1024, 1024, 256], P(('dp', 'rep')), may hold values from -0.59765625 to 0.59765625
- alphas: float32 [2, 256], replicated, may hold values from 0.5 to 4
- weights: bfloat16 [524288], replicated, may hold values from -0.125 to 0.125
- master: float32 [524288], P('dp'), may hold values from -2 to 2
- first_moment: float32 [524288], P('dp'), may hold values from -6 to 6
- second_moment: float32 [524288], P('dp'), may hold values from 0.05 to 2
Outputs:
- new_weights: bfloat16 [524288], replicated
- new_master: float32 [524288], P('dp')
- new_first: float32 [524288], P('dp')
- new_second: float32 [524288], P('dp')
All inputs are finite; a program needn't handle non-finite values.
Results may differ from a plain program's by a relative error of at most 0.0013.
Values may be sent and summed in bfloat16 or wider, within the bound.
No kernel may reach another device: no remote copies, remote signals or barrier semaphores. Data moves between devices by JAX's collectives and lax.ppermute only.
A program may use at most 32 MiB of HBM per device.

v0:
```python
import jax
import jax.numpy as jnp
from jax import lax
from jax.sharding import PartitionSpec as P

CH = 256
TAPS = 7
DILATION = 3


BIAS_ONE = 0.9999734386011124
BIAS_TWO = 0.09520785288629041


def snake(values, alpha):
    return values + jnp.sin(alpha * values) ** 2 / alpha


def clip_grads(clip, cot, alphas, weights):
    split = TAPS * CH * CH
    frames = clip.shape[0]
    w_dilated = weights[:split].reshape(TAPS * CH, CH)
    w_point = weights[split:].reshape(CH, CH)
    first = snake(clip.astype(jnp.float32), alphas[0]).astype(jnp.bfloat16)
    reach = DILATION * (TAPS // 2)
    padded = jnp.pad(first, ((reach, reach), (0, 0)))
    windows = jnp.concatenate(
        [padded[k * DILATION : k * DILATION + frames] for k in range(TAPS)], axis=1
    )
    hidden = jnp.dot(windows, w_dilated, preferred_element_type=jnp.float32)
    second = snake(hidden, alphas[1]).astype(jnp.bfloat16)
    point_grad = jnp.dot(second.T, cot, preferred_element_type=jnp.float32)
    back = jnp.dot(cot, w_point.T, preferred_element_type=jnp.float32)
    d_hidden = (back * (1.0 + jnp.sin(2.0 * alphas[1] * hidden))).astype(jnp.bfloat16)
    dilated_grad = jnp.dot(windows.T, d_hidden, preferred_element_type=jnp.float32)
    return jnp.concatenate([dilated_grad.reshape(-1), point_grad.reshape(-1)])


def adam_update(gradient, master, first_moment, second_moment):
    new_first = 0.9 * first_moment + 0.1 * gradient
    new_second = 0.999 * second_moment + 0.001 * gradient * gradient
    new_master = master - 0.001 * (new_first / BIAS_ONE) / (jnp.sqrt(new_second / BIAS_TWO) + 1e-08)
    return (new_master, new_first, new_second)


def shards(clips, cotangent, alphas, weights, master, first_moment, second_moment):
    local_grad = clip_grads(clips[0], cotangent[0], alphas, weights)
    block_sum = lax.psum_scatter(local_grad, "dp", scatter_dimension=0, tiled=True)
    gradient = lax.psum(block_sum, "rep")
    new_master, new_first, new_second = adam_update(gradient, master, first_moment, second_moment)
    new_weights = lax.all_gather(new_master.astype(jnp.bfloat16), "dp", axis=0, tiled=True)
    return (new_weights, new_master, new_first, new_second)


def solution(mesh):
    return jax.shard_map(
        shards,
        mesh=mesh,
        in_specs=(
            P(("dp", "rep"), None, None),
            P(("dp", "rep"), None, None),
            P(),
            P(),
            P("dp"),
            P("dp"),
            P("dp"),
        ),
        out_specs=(P(), P("dp"), P("dp"), P("dp")),
        check_vma=False,
    )
```

profile of v0, /device:TPU:1, one launch (start us, length us, event | category | flops | bytes accessed | tf_op | source)
XLA Modules:
  0.0 829.4 jit_solution(8527812653727232347)
XLA Ops:
  7.2 0.0 copy-start
  7.2 0.0 all-reduce.4.cloned.1.call-start
  7.2 0.8 broadcast_multiply_fusion
  8.0 4.6 fusion.4
  12.6 0.0 slice-start
  12.6 1.0 slice_dynamic-update-slice_fusion.5
  13.6 1.0 slice_dynamic-update-slice_fusion.4
  14.6 0.9 slice_dynamic-update-slice_fusion.3
  15.5 4.3 constant_dynamic-update-slice_fusion
  19.9 1.0 slice_dynamic-update-slice_fusion.2
  20.8 0.9 slice_dynamic-update-slice_fusion.1
  21.8 1.0 slice_dynamic-update-slice_fusion
  22.7 0.3 slice.63
  23.1 4.1 fusion.17
  27.2 6.7 convolution_bitcast_fusion
  33.9 0.9 copy.11
  34.9 0.3 copy-done.5
  35.2 3.9 convolution_bitcast_fusion.1
  39.1 0.0 copy-start.3
  39.1 0.0 copy-start.4
  39.1 0.1 copy.12
  39.3 1.4 pad_maximum_fusion
  40.7 0.0 all-reduce.4.cloned.1.call-update
  40.7 0.0 all-gather.2.cloned.1.call-start
  40.8 1.3 dynamic-slice
  42.7 563.9 %all-reduce.4.cloned.1.call-done = f32[524288]{0:T(1024)} async-done(((f32[524288]{0:T(1024)}), f32[524288]{0:T(1024)}) %all-reduce.4.cloned.1.call-update) | async-done | bytes 2097168
  606.6 0.8 dynamic-slice.1
  607.4 84.2 %psum.7 = f32[8192]{0:T(1024)S(1)} all-reduce(f32[8192]{0:T(1024)S(1)} %dynamic-slice.1), channel_id=1, replica_groups=mesh['dp'=64,'rep'=16] {'rep'}, use_global_device_ids=true, to_apply=%region_1.2 | all-reduce | flops 8192 | bytes 65536 | tf_op jit(solution)/shard_map/psum | solution.py:49
  691.7 0.7 fusion.15
  692.3 0.0 all-gather.2.cloned.1.call-update
  692.3 128.0 %all-gather.2.cloned.1.call-done = bf16[524288]{0:T(1024)(128)(2,1)} async-done(((bf16[8192]{0:T(1024)(128)(2,1)}), bf16[524288]{0:T(1024)(128)(2,1)}) %all-gather.2.cloned.1.call-update) | async-done | bytes 1048592 | tf_op jit(solution)/shard_map/all_gather | solution.py:51
  820.3 2.3 copy.21
  (12 shorter events, 0.1 us)
Async XLA Ops:
  7.2 20.1 %copy-start = (bf16[1,1024,256]{2,1,0:T(8,128)(2,1)S(1)}, bf16[1,1024,256]{2,1,0:T(8,128)(2,1)}, u32[]{:S(2)}) copy-start(bf16[1,1024,256]{2,1,0:T(8,128)(2,1)} %param.8) | copy-start | bytes 1572868
  7.2 8.3 %copy-start.1 = (bf16[1,1024,256]{2,1,0:T(8,128)(2,1)S(1)}, bf16[1,1024,256]{2,1,0:T(8,128)(2,1)}, u32[]{:S(2)}) copy-start(bf16[1,1024,256]{2,1,0:T(8,128)(2,1)} %param.7) | copy-start | bytes 1572868
  7.2 599.4 %all-reduce.4.cloned.1.call-start = ((), (), s32[]{:S(2)}) async-start(), calls=%async_computation.1 | async-start | bytes 4194304
  12.6 10.1 %slice-start = ((bf16[524288]{0:T(1024)(128)(2,1)}), bf16[458752]{0:T(1024)(128)(2,1)S(1)}, s32[]{:S(2)}) async-start(bf16[524288]{0:T(1024)(128)(2,1)} %param.10), calls=%async_computation.2 | async-start | bytes 1835008 | tf_op jit(solution)/shard_map/slice | solution.py:22
  14.6 8.5 %slice-start.1 = ((bf16[524288]{0:T(1024)(128)(2,1)}), bf16[65536]{0:T(1024)(128)(2,1)S(1)}, s32[]{:S(2)}) async-start(bf16[524288]{0:T(1024)(128)(2,1)} %param.10), calls=%async_computation.3 | async-start | bytes 262144 | tf_op jit(solution)/shard_map/slice | solution.py:23
  33.9 1.2 copy-start.5
  39.1 652.6 %copy-start.2 = (f32[8192]{0:T(1024)S(1)}, f32[8192]{0:T(1024)}, u32[]{:S(2)}) copy-start(f32[8192]{0:T(1024)} %param.11) | copy-start | bytes 98308
  39.1 652.6 %copy-start.3 = (f32[8192]{0:T(1024)S(1)}, f32[8192]{0:T(1024)}, u32[]{:S(2)}) copy-start(f32[8192]{0:T(1024)} %param.12) | copy-start | bytes 98308
  39.1 652.5 %copy-start.4 = (f32[8192]{0:T(1024)S(1)}, f32[8192]{0:T(1024)}, u32[]{:S(2)}) copy-start(f32[8192]{0:T(1024)} %param.13) | copy-start | bytes 98308
  40.7 779.6 %all-gather.2.cloned.1.call-start = ((), (), s32[]{:S(2)}) async-start(), calls=%async_computation | async-start | bytes 1064960 | tf_op jit(solution)/shard_map/all_gather | solution.py:51
Sparse Core Ops, SparseCore 0:
  40.9 565.7 all-reduce.3
  692.5 127.8 all-gather.1
where the time goes:
time: 830 us; the launch traced here: 829 us
  waiting for transfers between devices  692 us (83%)
  blocking collectives  84.2 us (10%)
  between operations  14.8 us (2%)
  matrix products  14.7 us (2%)
  local copies, waits for them, and re-layouts  11.8 us (1%)
  other arithmetic  11.8 us (1%)
    unnamed x3, waiting for transfers between devices  564 us
    all_gather x1, waiting for transfers between devices, shards(): lax.all_gather(new_master.astype(jnp.bfloat16), 'dp', axis=0, tiled=True)  128 us
    psum x1, blocking collectives, shards(): gradient = lax.psum(block_sum, 'rep')  84.2 us
  transfers between devices with their start and end apart: 2, of which 2 were waited for; matrix products, arithmetic and copies ran while one was open for 0% of the time, Pallas kernels for 0%

commit v1 on v0

v1 whole, which is shorter than its diff:
```python
import jax
import jax.numpy as jnp
from jax import lax
from jax.experimental import pallas as pl
from jax.experimental.pallas import tpu as pltpu
from jax.sharding import Mesh, PartitionSpec as P

CH = 256
TAPS = 7
DILATION = 3
PAD = 16
CHUNK = 256
BLOCK = 32

BIAS_ONE = 0.9999734386011124
BIAS_TWO = 0.09520785288629041

INV_PI = 0.3183098861837907
PI_A = 3.140625
PI_B = 9.67502593994140625e-4
PI_C = 1.509957990978376e-7


def reduced(t):
    n = jnp.round(t * INV_PI)
    return ((t - n * PI_A) - n * PI_B) - n * PI_C


def sine(r):
    z = r * r
    p = -2.4078282e-08
    for c in (2.75363800e-06, -1.98410853e-04, 8.33333284e-03, -1.66666672e-01):
        p = p * z + c
    return r + r * (z * p)


def cosine(r):
    z = r * r
    p = -2.62950522e-07
    for c in (2.47744738e-05, -1.38886506e-03, 4.16666605e-02, -0.5):
        p = p * z + c
    return 1.0 + z * p


def unit_kernel(core_ref, x_ref, cot_ref, al_ref, w_ref, keep_ref, send_ref, pad_ref, first_ref, second_ref):
    frames = x_ref.shape[0]
    even = core_ref[0] == 0
    a0 = al_ref[0:1, :]
    a1 = al_ref[1:2, :]
    r0 = 1.0 / a0
    r1 = 1.0 / a1
    pad_ref[0:PAD, :] = jnp.zeros((PAD, CH), jnp.float32)
    pad_ref[PAD + frames : 2 * PAD + frames, :] = jnp.zeros((PAD, CH), jnp.float32)
    for i in range(0, frames, CHUNK):
        x = x_ref[i : i + CHUNK, :].astype(jnp.float32)
        s = sine(reduced(a0 * x))
        first = (x + s * s * r0).astype(jnp.bfloat16)
        first_ref[i : i + CHUNK, :] = first
        pad_ref[PAD + i : PAD + i + CHUNK, :] = first.astype(jnp.float32)
    w_point = w_ref[TAPS * CH :, :]
    d_hidden = []
    for i in range(0, frames, CHUNK):
        hidden = None
        for k in range(TAPS):
            off = PAD + i + DILATION * (k - TAPS // 2)
            window = pad_ref[off : off + CHUNK, :].astype(jnp.bfloat16)
            part = jnp.dot(window, w_ref[k * CH : (k + 1) * CH, :], preferred_element_type=jnp.float32)
            hidden = part if hidden is None else hidden + part
        r = reduced(a1 * hidden)
        s = sine(r)
        second_ref[i : i + CHUNK, :] = (hidden + s * s * r1).astype(jnp.bfloat16)
        back = lax.dot_general(
            cot_ref[i : i + CHUNK, :], w_point, (((1,), (1,)), ((), ())), preferred_element_type=jnp.float32
        )
        d_hidden.append((back * (1.0 + 2.0 * s * cosine(r))).astype(jnp.bfloat16).astype(jnp.float32))
    for n, i in enumerate(range(0, frames, CHUNK)):
        pad_ref[PAD + i : PAD + i + CHUNK, :] = d_hidden[n]
    for k in range(TAPS + 1):
        if k < TAPS:
            off = PAD - DILATION * (k - TAPS // 2)
            left, right = first_ref[...], pad_ref[off : off + frames, :].astype(jnp.bfloat16)
        else:
            left, right = second_ref[...], cot_ref[...]
        grad = lax.dot_general(left, right, (((0,), (0,)), ((), ())), preferred_element_type=jnp.float32)
        for j in range(0, CH // BLOCK, 2):
            low = grad[j * BLOCK : (j + 1) * BLOCK, :]
            high = grad[(j + 1) * BLOCK : (j + 2) * BLOCK, :]
            slot = (k * (CH // BLOCK) + j) // 2
            place = (slot % 8) * 4 + slot // 8
            keep_ref[place] = jnp.where(even, low, high)
            send_ref[place] = jnp.where(even, high, low)


def clip_grads(clip, cot, alphas, weights, core):
    frames = clip.shape[0]
    vmem = pl.BlockSpec(memory_space=pltpu.VMEM)
    half = jax.ShapeDtypeStruct((32, BLOCK, CH), jnp.float32)
    return pl.pallas_call(
        unit_kernel,
        out_shape=(half, half),
        in_specs=[pl.BlockSpec(memory_space=pltpu.SMEM)] + [vmem] * 4,
        out_specs=(vmem, vmem),
        scratch_shapes=[
            pltpu.VMEM((frames + 2 * PAD, CH), jnp.float32),
            pltpu.VMEM((frames, CH), jnp.bfloat16),
            pltpu.VMEM((frames, CH), jnp.bfloat16),
        ],
        compiler_params=pltpu.CompilerParams(vmem_limit_bytes=40 << 20),
        cost_estimate=pl.CostEstimate(flops=2200000000, bytes_accessed=5 << 20, transcendentals=0),
    )(core, clip, cot, alphas, weights.reshape((TAPS + 1) * CH, CH))


def adam_update(gradient, master, first_moment, second_moment):
    new_first = 0.9 * first_moment + 0.1 * gradient
    new_second = 0.999 * second_moment + 0.001 * gradient * gradient
    new_master = master - 0.001 * (new_first / BIAS_ONE) / (jnp.sqrt(new_second / BIAS_TWO) + 1e-08)
    return (new_master, new_first, new_second)


SWAP = [(0, 1), (1, 0)]
CROSS = [(a * 4 + b, b * 4 + a) for a in range(4) for b in range(4)]


def shards(clips, cotangent, alphas, weights, master, first_moment, second_moment):
    core = lax.axis_index("c")
    there = lax.ppermute(jnp.stack([master, first_moment, second_moment]), ("zl", "x"), CROSS)
    keep, send = clip_grads(clips[0], cotangent[0], alphas, weights, core.reshape(1))
    part = keep + lax.ppermute(send, "c", SWAP)
    part = jnp.sum(lax.all_to_all(part, ("y", "x"), 0, 0, tiled=True), axis=0)
    for axis in ("zl", "zh"):
        part = jnp.broadcast_to(part[None], (4, BLOCK, CH))
        part = jnp.sum(lax.all_to_all(part, axis, 0, 0, tiled=True), axis=0)
    gradient = part.reshape(-1)
    mine = lax.ppermute(gradient, ("zl", "x"), CROSS)
    ahead, _, _ = adam_update(gradient, there[0], there[1], there[2])
    piece = ahead.astype(jnp.bfloat16).reshape(64, 128)
    piece = lax.all_to_all(jnp.broadcast_to(piece[None], (32, 64, 128)), ("y", "x"), 0, 0, tiled=True)
    other = lax.ppermute(piece, "c", SWAP)
    low = jnp.where(core == 0, piece, other)
    high = jnp.where(core == 0, other, piece)
    new_weights = jnp.stack([low, high], axis=1).reshape(8, 4, 2, 64, 128)
    new_weights = new_weights.transpose(1, 0, 2, 3, 4).reshape(-1)
    new_master, new_first, new_second = adam_update(mine, master, first_moment, second_moment)
    return (new_weights, new_master, new_first, new_second)


def solution(mesh):
    fine = Mesh(mesh.devices.reshape(4, 8, 2, 4, 4), ("zl", "y", "c", "zh", "x"))
    dp = ("zl", "y", "c")
    every = P(dp + ("zh", "x"), None, None)
    return jax.shard_map(
        shards,
        mesh=fine,
        in_specs=(every, every, P(), P(), P(dp), P(dp), P(dp)),
        out_specs=(P(), P(dp), P(dp), P(dp)),
        check_vma=False,
    )
```

time: 830 us -> 129 us (0.16)
  the two profiles are of different devices: /device:TPU:1 before, /device:TPU:4 now
where the time goes in v1:
time: 129 us; the launch traced here: 128 us
  blocking collectives  64.1 us (50%)
  starting transfers between devices  29.4 us (23%)
  waiting for transfers between devices  23.8 us (18%)
  local copies, waits for them, and re-layouts  4.71 us (4%)
  Pallas kernels  4.35 us (3%)
  other arithmetic  1.32 us (1%)
    all_to_all x1, blocking collectives, shards(): part = jnp.sum(lax.all_to_all(part, ('y', 'x'), 0, 0, tiled=True), axis=0)  44.5 us
    all_to_all x1, blocking collectives, shards(): lax.all_to_all(jnp.broadcast_to(piece[None], (32, 64, 128)), ('y', 'x'),...  19.5 us
    all_to_all x2, starting transfers between devices, shards(): part = jnp.sum(lax.all_to_all(part, axis, 0, 0, tiled=True), axis=0)  17.4 us
    all_to_all x2, waiting for transfers between devices, shards(): part = jnp.sum(lax.all_to_all(part, axis, 0, 0, tiled=True), axis=0)  14.8 us
    ppermute x1, waiting for transfers between devices, shards(): mine = lax.ppermute(gradient, ('zl', 'x'), CROSS)  6.36 us
    ppermute x1, starting transfers between devices, shards(): lax.ppermute(jnp.stack([master, first_moment, second_moment]), ('zl', 'x'...  4.77 us
    pallas_call x1, Pallas kernels, clip_grads(): pl.pallas_call(unit_kernel, out_shape=(half, half), in_specs=[pl.BlockSpe...  4.35 us
    ppermute x1, starting transfers between devices, shards(): mine = lax.ppermute(gradient, ('zl', 'x'), CROSS)  3.43 us
  transfers between devices with their start and end apart: 6, of which 4 were waited for; matrix products, arithmetic and copies ran while one was open for 1% of the time, Pallas kernels for 0%

profile of v1, /device:TPU:4, one launch (start us, length us, event | category | flops | bytes accessed | tf_op | source)
XLA Modules:
  0.0 128.5 jit_solution(12540486788192005372)
XLA Ops:
  0.6 0.0 copy-start
  0.6 0.0 copy-start.1
  0.7 1.5 %reshape.70.w_ref = bf16[2048,256]{1,0:T(8,128)(2,1)S(1)} reshape(bf16[524288]{0:T(1024)(128)(2,1)} %param.10) | data formatting | bytes 2097152 | tf_op jit(solution)/shard_map/reshape | solution.py:110
  2.2 0.0 copy-start.2
  2.2 0.0 copy-done
  2.2 0.7 copy-done.2
  2.9 4.4 %shard_map.102 = (f32[32,32,256]{2,1,0:T(8,128)S(1)}, f32[32,32,256]{2,1,0:T(8,128)S(1)}) custom-call(s32[1]{0:T(128)} %bitcast.5.core_ref, bf16[1024,256]{1,0:T(8,128)(2,1)S(1)} %bitcast.16, bf16[1024,256]{1,0:T(8,128)(2,1)S(1)} %bitcast.17, f32[2,256]{1,0:T(2,128)S(1)} %copy-done.2, bf16[2048,256]{1,0:T(8,128)(2,1)S(1)} %reshape.70.w_ref), custom_call_target="tpu_custom_call" | custom-call | flops 2200000000 | bytes 5242880 | tf_op jit(solution)/shard_map/pallas_call | solution.py:98
  7.2 1.9 %collective-permute-start.1 = (f32[32,32,256]{2,1,0:T(8,128)S(1)}, f32[32,32,256]{2,1,0:T(8,128)S(1)}, u32[]{:S(2)}, u32[]{:S(2)}) collective-permute-start(f32[32,32,256]{2,1,0:T(8,128)S(1)} %get-tuple-element.7), channel_id=1, source_target_pairs={{0,16},{16,0},{1,17},{17,1},{2,18},{18,2},{3,19},{19,3},{4,20},{20... | collective-permute-start | bytes 3145736 | tf_op jit(solution)/shard_map/ppermute | solution.py:128
  9.1 2.6 %collective-permute-done.1 = f32[32,32,256]{2,1,0:T(8,128)S(1)} collective-permute-done((f32[32,32,256]{2,1,0:T(8,128)S(1)}, f32[32,32,256]{2,1,0:T(8,128)S(1)}, u32[]{:S(2)}, u32[]{:S(2)}) %collective-permute-start.1) | collective-permute-done | bytes 1048608 | tf_op jit(solution)/shard_map/ppermute | solution.py:128
  11.8 0.2 add.33
  12.0 44.5 %all_to_all.20 = f32[32,32,256]{2,1,0:T(8,128)S(1)} all-to-all(f32[32,32,256]{2,1,0:T(8,128)S(1)} %add.33), channel_id=1, replica_groups=mesh['zl'=4,'y'=8,'c'=2,'zh'=4,'x'=4] {'y','x'}, dimensions={0} | all-to-all | bytes 2097152 | tf_op jit(solution)/shard_map/all_to_all | solution.py:129
  56.5 0.1 reduce_sum.27
  56.6 0.7 broadcast_in_dim.6
  57.2 3.5 %all-to-all-start.1 = ((f32[4,32,256]{2,1,0:T(8,128)}), f32[4,32,256]{2,1,0:T(8,128)S(1)}, u32[]{:S(2)}, u32[]{:S(2)}) async-start(f32[4,32,256]{2,1,0:T(8,128)} %broadcast_in_dim.6), calls=%async_computation.1 | async-start | bytes 262144 | tf_op jit(solution)/shard_map/all_to_all | solution.py:132
  60.7 0.1 pad_maximum_fusion
  60.8 4.8 %collective-permute-start = (f32[3,8192]{1,0:T(4,128)S(1)}, f32[3,8192]{1,0:T(4,128)S(1)}, u32[]{:S(2)}, u32[]{:S(2)}) collective-permute-start(f32[3,8192]{1,0:T(4,128)S(1)} %pad_maximum_fusion), channel_id=1, source_target_pairs={{0,0},{1,256},{2,512},{3,768},{256,1},{257,257},{258,513},{259,769... | collective-permute-start | bytes 294920 | tf_op jit(solution)/shard_map/ppermute | solution.py:126
  65.6 1.1 all-to-all-done.1
  66.7 0.7 broadcast_in_dim.7
  67.4 13.9 %all-to-all-start.2 = ((f32[4,32,256]{2,1,0:T(8,128)}), f32[4,32,256]{2,1,0:T(8,128)S(1)}, u32[]{:S(2)}, u32[]{:S(2)}) async-start(f32[4,32,256]{2,1,0:T(8,128)} %broadcast_in_dim.7), calls=%async_computation.2 | async-start | bytes 262144 | tf_op jit(solution)/shard_map/all_to_all | solution.py:132
  81.3 0.0 collective-permute-done
  81.3 0.1 slice_multiply_fusion.1
  81.4 13.7 %all-to-all-done.2 = f32[4,32,256]{2,1,0:T(8,128)S(1)} async-done(((f32[4,32,256]{2,1,0:T(8,128)}), f32[4,32,256]{2,1,0:T(8,128)S(1)}, u32[]{:S(2)}, u32[]{:S(2)}) %all-to-all-start.2) | async-done | bytes 131104 | tf_op jit(solution)/shard_map/all_to_all | solution.py:132
  95.2 0.1 broadcast_in_dim.8
  95.3 19.5 %all_to_all.21 = bf16[32,64,128]{2,1,0:T(8,128)(2,1)S(1)} all-to-all(bf16[32,64,128]{2,1,0:T(8,128)(2,1)S(1)} %broadcast_in_dim.8), channel_id=1, replica_groups=mesh['zl'=4,'y'=8,'c'=2,'zh'=4,'x'=4] {'y','x'}, dimensions={0} | all-to-all | bytes 1048576 | tf_op jit(solution)/shard_map/all_to_all | solution.py:137
  114.8 1.9 %collective-permute-start.2 = (bf16[32,64,128]{2,1,0:T(8,128)(2,1)S(1)}, bf16[32,64,128]{2,1,0:T(8,128)(2,1)S(1)}, u32[]{:S(2)}, u32[]{:S(2)}) collective-permute-start(bf16[32,64,128]{2,1,0:T(8,128)(2,1)S(1)} %all_to_all.21), channel_id=1, source_target_pairs={{0,16},{16,0},{1,17},{17,1},{2,18},{18,2},{3,19},{19,3},{4,20},{20... | collective-permute-start | bytes 1572872 | tf_op jit(solution)/shard_map/ppermute | solution.py:138
  116.8 3.4 %collective-permute-start.3 = (f32[8192]{0:T(1024)S(1)}, f32[8192]{0:T(1024)S(1)}, u32[]{:S(2)}, u32[]{:S(2)}) collective-permute-start(f32[8192]{0:T(1024)S(1)} %bitcast.28), channel_id=1, source_target_pairs={{0,0},{1,256},{2,512},{3,768},{256,1},{257,257},{258,513},{259,769... | collective-permute-start | bytes 98312 | tf_op jit(solution)/shard_map/ppermute | solution.py:134
  120.2 6.4 %collective-permute-done.3 = f32[8192]{0:T(1024)S(1)} collective-permute-done((f32[8192]{0:T(1024)S(1)}, f32[8192]{0:T(1024)S(1)}, u32[]{:S(2)}, u32[]{:S(2)}) %collective-permute-start.3) | collective-permute-done | bytes 32800 | tf_op jit(solution)/shard_map/ppermute | solution.py:134
  126.6 0.6 divide_subtract_fusion
  127.2 0.0 collective-permute-done.2
  127.2 0.1 broadcast_select_fusion.1
  127.3 0.1 maximum_bitcast_fusion
  127.4 1.1 copy.12
  (12 shorter events, 0.1 us)
Async XLA Ops:
  0.6 1.5 %copy-start = (bf16[1,1024,256]{2,1,0:T(8,128)(2,1)S(1)}, bf16[1,1024,256]{2,1,0:T(8,128)(2,1)}, u32[]{:S(2)}) copy-start(bf16[1,1024,256]{2,1,0:T(8,128)(2,1)} %param.7) | copy-start | bytes 1572868
  0.6 1.5 %copy-start.1 = (bf16[1,1024,256]{2,1,0:T(8,128)(2,1)S(1)}, bf16[1,1024,256]{2,1,0:T(8,128)(2,1)}, u32[]{:S(2)}) copy-start(bf16[1,1024,256]{2,1,0:T(8,128)(2,1)} %param.8) | copy-start | bytes 1572868
  2.2 0.7 copy-start.2
  7.2 4.6 %collective-permute-start.1 = (f32[32,32,256]{2,1,0:T(8,128)S(1)}, f32[32,32,256]{2,1,0:T(8,128)S(1)}, u32[]{:S(2)}, u32[]{:S(2)}) collective-permute-start(f32[32,32,256]{2,1,0:T(8,128)S(1)} %get-tuple-element.7), channel_id=1, source_target_pairs={{0,16},{16,0},{1,17},{17,1},{2,18},{18,2},{3,19},{19,3},{4,20},{20... | collective-permute-start | bytes 3145736 | tf_op jit(solution)/shard_map/ppermute | solution.py:128
  57.2 3.5 %copy-start.3 = (f32[8192]{0:T(1024)S(1)}, f32[8192]{0:T(1024)}, u32[]{:S(2)}) copy-start(f32[8192]{0:T(1024)} %param.13) | copy-start | bytes 98308
  57.2 3.5 %copy-start.4 = (f32[8192]{0:T(1024)S(1)}, f32[8192]{0:T(1024)}, u32[]{:S(2)}) copy-start(f32[8192]{0:T(1024)} %param.12) | copy-start | bytes 98308
  57.2 3.5 %copy-start.5 = (f32[8192]{0:T(1024)S(1)}, f32[8192]{0:T(1024)}, u32[]{:S(2)}) copy-start(f32[8192]{0:T(1024)} %param.11) | copy-start | bytes 98308
  57.2 9.5 %all-to-all-start.1 = ((f32[4,32,256]{2,1,0:T(8,128)}), f32[4,32,256]{2,1,0:T(8,128)S(1)}, u32[]{:S(2)}, u32[]{:S(2)}) async-start(f32[4,32,256]{2,1,0:T(8,128)} %broadcast_in_dim.6), calls=%async_computation.1 | async-start | bytes 262144 | tf_op jit(solution)/shard_map/all_to_all | solution.py:132
  60.8 20.5 %collective-permute-start = (f32[3,8192]{1,0:T(4,128)S(1)}, f32[3,8192]{1,0:T(4,128)S(1)}, u32[]{:S(2)}, u32[]{:S(2)}) collective-permute-start(f32[3,8192]{1,0:T(4,128)S(1)} %pad_maximum_fusion), channel_id=1, source_target_pairs={{0,0},{1,256},{2,512},{3,768},{256,1},{257,257},{258,513},{259,769... | collective-permute-start | bytes 294920 | tf_op jit(solution)/shard_map/ppermute | solution.py:126
  67.4 27.7 %all-to-all-start.2 = ((f32[4,32,256]{2,1,0:T(8,128)}), f32[4,32,256]{2,1,0:T(8,128)S(1)}, u32[]{:S(2)}, u32[]{:S(2)}) async-start(f32[4,32,256]{2,1,0:T(8,128)} %broadcast_in_dim.7), calls=%async_computation.2 | async-start | bytes 262144 | tf_op jit(solution)/shard_map/all_to_all | solution.py:132
  114.8 12.4 %collective-permute-start.2 = (bf16[32,64,128]{2,1,0:T(8,128)(2,1)S(1)}, bf16[32,64,128]{2,1,0:T(8,128)(2,1)S(1)}, u32[]{:S(2)}, u32[]{:S(2)}) collective-permute-start(bf16[32,64,128]{2,1,0:T(8,128)(2,1)S(1)} %all_to_all.21), channel_id=1, source_target_pairs={{0,16},{16,0},{1,17},{17,1},{2,18},{18,2},{3,19},{19,3},{4,20},{20... | collective-permute-start | bytes 1572872 | tf_op jit(solution)/shard_map/ppermute | solution.py:138
  116.8 9.8 %collective-permute-start.3 = (f32[8192]{0:T(1024)S(1)}, f32[8192]{0:T(1024)S(1)}, u32[]{:S(2)}, u32[]{:S(2)}) collective-permute-start(f32[8192]{0:T(1024)S(1)} %bitcast.28), channel_id=1, source_target_pairs={{0,0},{1,256},{2,512},{3,768},{256,1},{257,257},{258,513},{259,769... | collective-permute-start | bytes 98312 | tf_op jit(solution)/shard_map/ppermute | solution.py:134

commit v2 on v1

--- a/solution.py
+++ b/solution.py
@@ -86,9 +86,8 @@
             low = grad[j * BLOCK : (j + 1) * BLOCK, :]
             high = grad[(j + 1) * BLOCK : (j + 2) * BLOCK, :]
             slot = (k * (CH // BLOCK) + j) // 2
-            place = (slot % 8) * 4 + slot // 8
-            keep_ref[place] = jnp.where(even, low, high)
-            send_ref[place] = jnp.where(even, high, low)
+            keep_ref[slot] = jnp.where(even, low, high)
+            send_ref[slot] = jnp.where(even, high, low)
 
 
 def clip_grads(clip, cot, alphas, weights, core):
@@ -118,29 +117,32 @@
 
 
 SWAP = [(0, 1), (1, 0)]
-CROSS = [(a * 4 + b, b * 4 + a) for a in range(4) for b in range(4)]
+
+
+def packed(values):
+    root = jnp.sqrt(jnp.abs(values))
+    return jnp.where(values < 0, -root, root).astype(jnp.float16)
+
+
+def unpacked(roots):
+    roots = roots.astype(jnp.float32)
+    return roots * jnp.abs(roots)
 
 
 def shards(clips, cotangent, alphas, weights, master, first_moment, second_moment):
     core = lax.axis_index("c")
-    there = lax.ppermute(jnp.stack([master, first_moment, second_moment]), ("zl", "x"), CROSS)
     keep, send = clip_grads(clips[0], cotangent[0], alphas, weights, core.reshape(1))
-    part = keep + lax.ppermute(send, "c", SWAP)
-    part = jnp.sum(lax.all_to_all(part, ("y", "x"), 0, 0, tiled=True), axis=0)
-    for axis in ("zl", "zh"):
-        part = jnp.broadcast_to(part[None], (4, BLOCK, CH))
-        part = jnp.sum(lax.all_to_all(part, axis, 0, 0, tiled=True), axis=0)
-    gradient = part.reshape(-1)
-    mine = lax.ppermute(gradient, ("zl", "x"), CROSS)
-    ahead, _, _ = adam_update(gradient, there[0], there[1], there[2])
-    piece = ahead.astype(jnp.bfloat16).reshape(64, 128)
-    piece = lax.all_to_all(jnp.broadcast_to(piece[None], (32, 64, 128)), ("y", "x"), 0, 0, tiled=True)
+    part = packed(keep + lax.ppermute(send, "c", SWAP))
+    part = lax.all_to_all(part.reshape(128, BLOCK // 4, CH), ("zl", "y", "x"), 0, 0, tiled=True)
+    part = jnp.broadcast_to(jnp.sum(unpacked(part), axis=0)[None], (16, BLOCK // 4, CH))
+    part = lax.all_to_all(part, ("zh", "x"), 0, 0, tiled=True)
+    gradient = jnp.sum(part.reshape(4, BLOCK, CH), axis=0).reshape(-1)
+    new_master, new_first, new_second = adam_update(gradient, master, first_moment, second_moment)
+    piece = new_master.astype(jnp.bfloat16).reshape(64, 128)
+    piece = lax.all_to_all(jnp.broadcast_to(piece[None], (32, 64, 128)), ("zl", "y"), 0, 0, tiled=True)
     other = lax.ppermute(piece, "c", SWAP)
-    low = jnp.where(core == 0, piece, other)
-    high = jnp.where(core == 0, other, piece)
-    new_weights = jnp.stack([low, high], axis=1).reshape(8, 4, 2, 64, 128)
-    new_weights = new_weights.transpose(1, 0, 2, 3, 4).reshape(-1)
-    new_master, new_first, new_second = adam_update(mine, master, first_moment, second_moment)
+    place = lax.broadcasted_iota(jnp.int32, (32, 2, 64, 128), 1)
+    new_weights = jnp.where(place == core, piece[:, None], other[:, None]).reshape(-1)
     return (new_weights, new_master, new_first, new_second)
 
 

time: 129 us -> 108 us (0.84)
  the two profiles are of different devices: /device:TPU:4 before, /device:TPU:1 now
where the time goes in v2:
time: 108 us
  blocking collectives  70.3 us (65%)
  starting transfers between devices  23.3 us (22%)
  Pallas kernels  4.35 us (4%)
  waiting for transfers between devices  3.76 us (3%)
  local copies, waits for them, and re-layouts  3.05 us (3%)
  other arithmetic  2.44 us (2%)
    all_to_all x1, blocking collectives, shards(): part = lax.all_to_all(part, ('zh', 'x'), 0, 0, tiled=True)  28.9 us
    all_to_all x1, blocking collectives, shards(): lax.all_to_all(part.reshape(128, BLOCK // 4, CH), ('zl', 'y', 'x'), 0, 0,...  24.5 us
    all_to_all x1, blocking collectives, shards(): lax.all_to_all(jnp.broadcast_to(piece[None], (32, 64, 128)), ('zl', 'y'),...  16.9 us
    ppermute x1, starting transfers between devices, shards(): part = packed(keep + lax.ppermute(send, 'c', SWAP))  16 us
    ppermute x1, starting transfers between devices, shards(): other = lax.ppermute(piece, 'c', SWAP)  7.31 us
    pallas_call x1, Pallas kernels, clip_grads(): pl.pallas_call(unit_kernel, out_shape=(half, half), in_specs=[pl.BlockSpe...  4.35 us
    ppermute x1, waiting for transfers between devices, shards(): part = packed(keep + lax.ppermute(send, 'c', SWAP))  2.26 us
  transfers between devices with their start and end apart: 2, of which 2 were waited for; matrix products, arithmetic and copies ran while one was open for 0% of the time, Pallas kernels for 0%

profile of v2, /device:TPU:1, one launch (start us, length us, event | category | flops | bytes accessed | tf_op | source)
XLA Modules:
  0.0 107.9 jit_solution(14738089505204280559)
XLA Ops:
  0.6 0.0 copy-start
  0.6 0.0 copy-start.1
  0.7 1.5 %reshape.33.w_ref = bf16[2048,256]{1,0:T(8,128)(2,1)S(1)} reshape(bf16[524288]{0:T(1024)(128)(2,1)} %param.10) | data formatting | bytes 2097152 | tf_op jit(solution)/shard_map/reshape | solution.py:109
  2.2 0.0 copy-start.2
  2.2 0.0 copy-done
  2.2 0.0 copy-done.1
  2.2 0.7 copy-done.2
  2.9 4.3 %shard_map.102 = (f32[32,32,256]{2,1,0:T(8,128)S(1)}, f32[32,32,256]{2,1,0:T(8,128)S(1)}) custom-call(s32[1]{0:T(128)} %bitcast.core_ref, bf16[1024,256]{1,0:T(8,128)(2,1)S(1)} %bitcast.12, bf16[1024,256]{1,0:T(8,128)(2,1)S(1)} %bitcast.13, f32[2,256]{1,0:T(2,128)S(1)} %copy-done.2, bf16[2048,256]{1,0:T(8,128)(2,1)S(1)} %reshape.33.w_ref), custom_call_target="tpu_custom_call" | custom-call | flops 2200000000 | bytes 5242880 | tf_op jit(solution)/shard_map/pallas_call | solution.py:97
  7.2 16.0 %collective-permute-start = (f32[32,32,256]{2,1,0:T(8,128)S(1)}, f32[32,32,256]{2,1,0:T(8,128)S(1)}, u32[]{:S(2)}, u32[]{:S(2)}) collective-permute-start(f32[32,32,256]{2,1,0:T(8,128)S(1)} %get-tuple-element.7), channel_id=1, source_target_pairs={{0,16},{16,0},{1,17},{17,1},{2,18},{18,2},{3,19},{19,3},{4,20},{20... | collective-permute-start | bytes 3145736 | tf_op jit(solution)/shard_map/ppermute | solution.py:135
  23.2 2.3 %collective-permute-done = f32[32,32,256]{2,1,0:T(8,128)S(1)} collective-permute-done((f32[32,32,256]{2,1,0:T(8,128)S(1)}, f32[32,32,256]{2,1,0:T(8,128)S(1)}, u32[]{:S(2)}, u32[]{:S(2)}) %collective-permute-start) | collective-permute-done | bytes 1048608 | tf_op jit(solution)/shard_map/ppermute | solution.py:135
  25.5 0.5 fusion
  26.0 24.5 %all_to_all.15 = f16[128,8,256]{2,1,0:T(8,128)(2,1)S(1)} all-to-all(f16[128,8,256]{2,1,0:T(8,128)(2,1)S(1)} %bitcast.14), channel_id=1, replica_groups=mesh['zl'=4,'y'=8,'c'=2,'zh'=4,'x'=4] {'zl','y','x'}, dimensions={0} | all-to-all | bytes 1048576 | tf_op jit(solution)/shard_map/all_to_all | solution.py:136
  50.5 0.2 fusion.1
  50.7 28.9 %all_to_all.16 = f32[16,8,256]{2,1,0:T(8,128)S(1)} all-to-all(f32[16,8,256]{2,1,0:T(8,128)S(1)} %broadcast_in_dim.31), channel_id=1, replica_groups=mesh['zl'=4,'y'=8,'c'=2,'zh'=4,'x'=4] {'zh','x'}, dimensions={0} | all-to-all | bytes 262144 | tf_op jit(solution)/shard_map/all_to_all | solution.py:138
  79.6 0.0 copy-start.5
  79.6 0.0 copy-start.3
  79.6 0.0 copy-start.4
  79.6 0.7 copy-done.5
  80.3 0.0 copy-done.3
  80.4 0.0 copy-done.4
  80.4 0.6 convert_bitcast_fusion
  81.0 0.1 broadcast_in_dim.33
  81.1 16.9 %all_to_all.17 = bf16[32,64,128]{2,1,0:T(8,128)(2,1)S(1)} all-to-all(bf16[32,64,128]{2,1,0:T(8,128)(2,1)S(1)} %broadcast_in_dim.33), channel_id=1, replica_groups=mesh['zl'=4,'y'=8,'c'=2,'zh'=4,'x'=4] {'zl','y'}, dimensions={0} | all-to-all | bytes 1048576 | tf_op jit(solution)/shard_map/all_to_all | solution.py:142
  98.0 7.3 %collective-permute-start.1 = (bf16[32,64,128]{2,1,0:T(8,128)(2,1)S(1)}, bf16[32,64,128]{2,1,0:T(8,128)(2,1)S(1)}, u32[]{:S(2)}, u32[]{:S(2)}) collective-permute-start(bf16[32,64,128]{2,1,0:T(8,128)(2,1)S(1)} %all_to_all.17), channel_id=1, source_target_pairs={{0,16},{16,0},{1,17},{17,1},{2,18},{18,2},{3,19},{19,3},{4,20},{20... | collective-permute-start | bytes 1572872 | tf_op jit(solution)/shard_map/ppermute | solution.py:143
  105.3 1.5 %collective-permute-done.1 = bf16[32,64,128]{2,1,0:T(8,128)(2,1)S(1)} collective-permute-done((bf16[32,64,128]{2,1,0:T(8,128)(2,1)S(1)}, bf16[32,64,128]{2,1,0:T(8,128)(2,1)S(1)}, u32[]{:S(2)}, u32[]{:S(2)}) %collective-permute-start.1) | collective-permute-done | bytes 524320 | tf_op jit(solution)/shard_map/ppermute | solution.py:143
  106.8 1.1 %broadcast_select_fusion = bf16[32,2,64,128]{3,2,1,0:T(8,128)(2,1)} fusion(pred[2]{0:T(512)(128)(4,1)S(1)} %iota_compare_fusion, bf16[32,64,128]{2,1,0:T(8,128)(2,1)S(1)} %collective-permute-done.1, bf16[32,64,128]{2,1,0:T(8,128)(2,1)S(1)} %all_to_all.17), kind=kLoop, calls=%fused_computation.4 | loop fusion | flops 524288 | bytes 2097154 | tf_op jit(solution)/shard_map/jit(_where)/select_n | solution.py:145
  (4 shorter events, 0.1 us)
Async XLA Ops:
  0.6 1.5 %copy-start = (bf16[1,1024,256]{2,1,0:T(8,128)(2,1)S(1)}, bf16[1,1024,256]{2,1,0:T(8,128)(2,1)}, u32[]{:S(2)}) copy-start(bf16[1,1024,256]{2,1,0:T(8,128)(2,1)} %param.7) | copy-start | bytes 1572868
  0.6 1.5 %copy-start.1 = (bf16[1,1024,256]{2,1,0:T(8,128)(2,1)S(1)}, bf16[1,1024,256]{2,1,0:T(8,128)(2,1)}, u32[]{:S(2)}) copy-start(bf16[1,1024,256]{2,1,0:T(8,128)(2,1)} %param.8) | copy-start | bytes 1572868
  2.2 0.7 copy-start.2
  7.2 18.3 %collective-permute-start = (f32[32,32,256]{2,1,0:T(8,128)S(1)}, f32[32,32,256]{2,1,0:T(8,128)S(1)}, u32[]{:S(2)}, u32[]{:S(2)}) collective-permute-start(f32[32,32,256]{2,1,0:T(8,128)S(1)} %get-tuple-element.7), channel_id=1, source_target_pairs={{0,16},{16,0},{1,17},{17,1},{2,18},{18,2},{3,19},{19,3},{4,20},{20... | collective-permute-start | bytes 3145736 | tf_op jit(solution)/shard_map/ppermute | solution.py:135
  79.6 0.8 copy-start.5
  79.6 0.8 copy-start.3
  79.6 0.8 copy-start.4
  98.0 8.8 %collective-permute-start.1 = (bf16[32,64,128]{2,1,0:T(8,128)(2,1)S(1)}, bf16[32,64,128]{2,1,0:T(8,128)(2,1)S(1)}, u32[]{:S(2)}, u32[]{:S(2)}) collective-permute-start(bf16[32,64,128]{2,1,0:T(8,128)(2,1)S(1)} %all_to_all.17), channel_id=1, source_target_pairs={{0,16},{16,0},{1,17},{17,1},{2,18},{18,2},{3,19},{19,3},{4,20},{20... | collective-permute-start | bytes 1572872 | tf_op jit(solution)/shard_map/ppermute | solution.py:143

commit v3 on v2

--- a/solution.py
+++ b/solution.py
@@ -11,6 +11,7 @@
 PAD = 16
 CHUNK = 256
 BLOCK = 32
+QUARTER = BLOCK // 4
 
 BIAS_ONE = 0.9999734386011124
 BIAS_TWO = 0.09520785288629041
@@ -42,22 +43,42 @@
     return 1.0 + z * p
 
 
-def unit_kernel(core_ref, x_ref, cot_ref, al_ref, w_ref, keep_ref, send_ref, pad_ref, first_ref, second_ref):
+def unit_kernel(
+    core_ref, x_hbm, cot_hbm, al_hbm, w_hbm, keep_ref, send_ref,
+    x_ref, cot_ref, al_ref, flat_ref, wide_ref, w_ref, pad_ref, first_ref, second_ref, sems,
+):
+    copies = [
+        pltpu.make_async_copy(source, target, sems.at[n])
+        for n, (source, target) in enumerate(
+            ((al_hbm, al_ref), (x_hbm, x_ref), (w_hbm, flat_ref), (cot_hbm, cot_ref))
+        )
+    ]
+    for copy in copies:
+        copy.start()
     frames = x_ref.shape[0]
+    rows = w_ref.shape[0]
     even = core_ref[0] == 0
+    pad_ref[0:PAD, :] = jnp.zeros((PAD, CH), jnp.float32)
+    pad_ref[PAD + frames : 2 * PAD + frames, :] = jnp.zeros((PAD, CH), jnp.float32)
+    copies[0].wait()
     a0 = al_ref[0:1, :]
     a1 = al_ref[1:2, :]
     r0 = 1.0 / a0
     r1 = 1.0 / a1
-    pad_ref[0:PAD, :] = jnp.zeros((PAD, CH), jnp.float32)
-    pad_ref[PAD + frames : 2 * PAD + frames, :] = jnp.zeros((PAD, CH), jnp.float32)
+    copies[1].wait()
     for i in range(0, frames, CHUNK):
         x = x_ref[i : i + CHUNK, :].astype(jnp.float32)
         s = sine(reduced(a0 * x))
         first = (x + s * s * r0).astype(jnp.bfloat16)
         first_ref[i : i + CHUNK, :] = first
         pad_ref[PAD + i : PAD + i + CHUNK, :] = first.astype(jnp.float32)
+    copies[2].wait()
+    wide_ref[...] = flat_ref[...].astype(jnp.float32)
+    for side in range(2):
+        half = wide_ref[pl.ds(side, rows, stride=2), :]
+        w_ref[:, side * 128 : (side + 1) * 128] = half.astype(jnp.bfloat16)
     w_point = w_ref[TAPS * CH :, :]
+    copies[3].wait()
     d_hidden = []
     for i in range(0, frames, CHUNK):
         hidden = None
@@ -83,35 +104,46 @@
             left, right = second_ref[...], cot_ref[...]
         grad = lax.dot_general(left, right, (((0,), (0,)), ((), ())), preferred_element_type=jnp.float32)
         for j in range(0, CH // BLOCK, 2):
-            low = grad[j * BLOCK : (j + 1) * BLOCK, :]
-            high = grad[(j + 1) * BLOCK : (j + 2) * BLOCK, :]
             slot = (k * (CH // BLOCK) + j) // 2
-            keep_ref[slot] = jnp.where(even, low, high)
-            send_ref[slot] = jnp.where(even, high, low)
+            for q in range(4):
+                row = j * BLOCK + q * QUARTER
+                low = grad[row : row + QUARTER, :]
+                high = grad[row + BLOCK : row + BLOCK + QUARTER, :]
+                place = (slot % 8) * 4 + q, pl.ds(slot // 8 * QUARTER, QUARTER)
+                keep_ref[place] = jnp.where(even, low, high)
+                send_ref[place] = jnp.where(even, high, low)
 
 
 def clip_grads(clip, cot, alphas, weights, core):
     frames = clip.shape[0]
+    rows = (TAPS + 1) * CH
     vmem = pl.BlockSpec(memory_space=pltpu.VMEM)
-    half = jax.ShapeDtypeStruct((32, BLOCK, CH), jnp.float32)
+    half = jax.ShapeDtypeStruct((32, 4 * QUARTER, CH), jnp.float32)
     return pl.pallas_call(
         unit_kernel,
         out_shape=(half, half),
-        in_specs=[pl.BlockSpec(memory_space=pltpu.SMEM)] + [vmem] * 4,
+        in_specs=[pl.BlockSpec(memory_space=pltpu.SMEM)] + [pl.BlockSpec(memory_space=pltpu.HBM)] * 4,
         out_specs=(vmem, vmem),
         scratch_shapes=[
+            pltpu.VMEM((frames, CH), jnp.bfloat16),
+            pltpu.VMEM((frames, CH), jnp.bfloat16),
+            pltpu.VMEM((2, CH), jnp.float32),
+            pltpu.VMEM((2 * rows, 128), jnp.bfloat16),
+            pltpu.VMEM((2 * rows, 128), jnp.float32),
+            pltpu.VMEM((rows, CH), jnp.bfloat16),
             pltpu.VMEM((frames + 2 * PAD, CH), jnp.float32),
             pltpu.VMEM((frames, CH), jnp.bfloat16),
             pltpu.VMEM((frames, CH), jnp.bfloat16),
+            pltpu.SemaphoreType.DMA((4,)),
         ],
         compiler_params=pltpu.CompilerParams(vmem_limit_bytes=40 << 20),
         cost_estimate=pl.CostEstimate(flops=2200000000, bytes_accessed=5 << 20, transcendentals=0),
-    )(core, clip, cot, alphas, weights.reshape((TAPS + 1) * CH, CH))
+    )(core, *[pltpu.with_memory_space_constraint(v, pltpu.HBM) for v in (clip, cot, alphas, weights.reshape(2 * rows, 128))])
 
 
-def adam_update(gradient, master, first_moment, second_moment):
-    new_first = 0.9 * first_moment + 0.1 * gradient
-    new_second = 0.999 * second_moment + 0.001 * gradient * gradient
+def adam_update(gradient, master, first_part, second_part):
+    new_first = first_part + 0.1 * gradient
+    new_second = second_part + 0.001 * gradient * gradient
     new_master = master - 0.001 * (new_first / BIAS_ONE) / (jnp.sqrt(new_second / BIAS_TWO) + 1e-08)
     return (new_master, new_first, new_second)
 
@@ -132,12 +164,15 @@
 def shards(clips, cotangent, alphas, weights, master, first_moment, second_moment):
     core = lax.axis_index("c")
     keep, send = clip_grads(clips[0], cotangent[0], alphas, weights, core.reshape(1))
-    part = packed(keep + lax.ppermute(send, "c", SWAP))
-    part = lax.all_to_all(part.reshape(128, BLOCK // 4, CH), ("zl", "y", "x"), 0, 0, tiled=True)
-    part = jnp.broadcast_to(jnp.sum(unpacked(part), axis=0)[None], (16, BLOCK // 4, CH))
+    ready = jnp.concatenate([master, 0.9 * first_moment, 0.999 * second_moment])
+    recv, ready = lax.optimization_barrier((lax.ppermute(send, "c", SWAP), ready))
+    part = lax.all_to_all(packed(keep + recv), ("y", "x"), 0, 0, tiled=True)
+    part = jnp.sum(unpacked(part), axis=0).reshape(4, QUARTER, CH)
+    part = jnp.sum(lax.all_to_all(part, "zl", 0, 0, tiled=True), axis=0)
+    part = jnp.broadcast_to(part[None], (16, QUARTER, CH))
     part = lax.all_to_all(part, ("zh", "x"), 0, 0, tiled=True)
     gradient = jnp.sum(part.reshape(4, BLOCK, CH), axis=0).reshape(-1)
-    new_master, new_first, new_second = adam_update(gradient, master, first_moment, second_moment)
+    new_master, new_first, new_second = adam_update(gradient, *jnp.split(ready, 3))
     piece = new_master.astype(jnp.bfloat16).reshape(64, 128)
     piece = lax.all_to_all(jnp.broadcast_to(piece[None], (32, 64, 128)), ("zl", "y"), 0, 0, tiled=True)
     other = lax.ppermute(piece, "c", SWAP)

time: 108 us -> 109 us (level)
  local copies, waits for them, and re-layouts: 3.05 us -> 0.16 us
  blocking collectives: 70.3 us -> 73 us
  Pallas kernels: 4.35 us -> 5.89 us
    all_to_all x1 -> x2, blocking collectives: 24.5 us -> 26.5 us  [the longest x1 19.6 us: shards(): part = lax.all_to_all(packed(keep + recv), ('y', 'x'), 0, 0, tiled=True)]
    pallas_call x1, Pallas kernels: 4.35 us -> 5.89 us  [clip_grads(): pl.pallas_call(unit_kernel, out_shape=(half, half), in_specs=[pl.BlockSpe...]
    reshape x1, local copies, waits for them, and re-layouts: 1.5 us -> 0.01 us  [shards(): gradient = jnp.sum(part.reshape(4, BLOCK, CH), axis=0).reshape(-1)]
    unnamed x13 -> x7, local copies, waits for them, and re-layouts: 1.42 us -> 0.03 us
  transfers between devices with their start and end apart: 2 -> 2, of which waited for: 2 -> 2; matrix products, arithmetic and copies ran while one was open for 0% -> 1% of each run, Pallas kernels for 0% -> 0%
where the time goes in v3:
time: 109 us
  blocking collectives  73 us (67%)
  starting transfers between devices  23.7 us (22%)
  Pallas kernels  5.89 us (5%)
  waiting for transfers between devices  3.02 us (3%)
  other arithmetic  2.45 us (2%)
    all_to_all x1, blocking collectives, shards(): part = lax.all_to_all(part, ('zh', 'x'), 0, 0, tiled=True)  29.9 us
    all_to_all x1, blocking collectives, shards(): part = lax.all_to_all(packed(keep + recv), ('y', 'x'), 0, 0, tiled=True)  19.6 us
    all_to_all x1, blocking collectives, shards(): lax.all_to_all(jnp.broadcast_to(piece[None], (32, 64, 128)), ('zl', 'y'),...  16.6 us
    ppermute x1, starting transfers between devices, shards(): lax.ppermute(send, 'c', SWAP)  16 us
    ppermute x1, starting transfers between devices, shards(): other = lax.ppermute(piece, 'c', SWAP)  7.68 us
    all_to_all x1, blocking collectives, shards(): part = jnp.sum(lax.all_to_all(part, 'zl', 0, 0, tiled=True), axis=0)  6.86 us
    pallas_call x1, Pallas kernels, clip_grads(): pl.pallas_call(unit_kernel, out_shape=(half, half), in_specs=[pl.BlockSpe...  5.89 us
    ppermute x1, waiting for transfers between devices, shards(): lax.ppermute(send, 'c', SWAP)  2.2 us
  transfers between devices with their start and end apart: 2, of which 2 were waited for; matrix products, arithmetic and copies ran while one was open for 1% of the time, Pallas kernels for 0%

profile of v3, /device:TPU:1, one launch (start us, length us, event | category | flops | bytes accessed | tf_op | source)
XLA Modules:
  0.0 109.0 jit_solution(9715698799953808561)
XLA Ops:
  0.6 0.0 copy-start
  0.6 0.0 copy-start.1
  0.7 5.9 %shard_map.102 = (f32[32,32,256]{2,1,0:T(8,128)S(1)}, f32[32,32,256]{2,1,0:T(8,128)S(1)}) custom-call(s32[1]{0:T(128)} %bitcast.core_ref, bf16[1024,256]{1,0:T(8,128)(2,1)} %bitcast.33, bf16[1024,256]{1,0:T(8,128)(2,1)} %bitcast.34, f32[2,256]{1,0:T(2,128)} %al_hbm.1, bf16[4096,128]{1,0:T(8,128)(2,1)} %bitcast.32), custom_call_target="tpu_custom_call" | custom-call | flops 2200000000 | bytes 5242880 | tf_op jit(solution)/shard_map/pallas_call | solution.py:122
  6.6 0.0 copy-start.2
  6.6 16.0 %collective-permute-start = (f32[32,32,256]{2,1,0:T(8,128)S(1)}, f32[32,32,256]{2,1,0:T(8,128)S(1)}, u32[]{:S(2)}, u32[]{:S(2)}) collective-permute-start(f32[32,32,256]{2,1,0:T(8,128)S(1)} %get-tuple-element.8), channel_id=1, source_target_pairs={{0,16},{16,0},{1,17},{17,1},{2,18},{18,2},{3,19},{19,3},{4,20},{20... | collective-permute-start | bytes 3145736 | tf_op jit(solution)/shard_map/ppermute | solution.py:168
  22.6 0.0 copy-done
  22.6 0.0 copy-done.1
  22.6 0.0 copy-done.2
  22.7 2.2 %collective-permute-done = f32[32,32,256]{2,1,0:T(8,128)S(1)} collective-permute-done((f32[32,32,256]{2,1,0:T(8,128)S(1)}, f32[32,32,256]{2,1,0:T(8,128)S(1)}, u32[]{:S(2)}, u32[]{:S(2)}) %collective-permute-start) | collective-permute-done | bytes 1048608 | tf_op jit(solution)/shard_map/ppermute | solution.py:168
  24.9 0.5 fusion
  25.3 19.6 %all_to_all.20 = f16[32,32,256]{2,1,0:T(8,128)(2,1)S(1)} all-to-all(f16[32,32,256]{2,1,0:T(8,128)(2,1)S(1)} %fusion), channel_id=1, replica_groups=mesh['zl'=4,'y'=8,'c'=2,'zh'=4,'x'=4] {'y','x'}, dimensions={0} | all-to-all | bytes 1048576 | tf_op jit(solution)/shard_map/all_to_all | solution.py:169
  45.0 0.1 fusion.1
  45.1 6.9 %all_to_all.21 = f32[4,8,256]{2,1,0:T(8,128)S(1)} all-to-all(f32[4,8,256]{2,1,0:T(8,128)S(1)} %bitcast.31), channel_id=1, replica_groups=mesh['zl'=4,'y'=8,'c'=2,'zh'=4,'x'=4] {'zl'}, dimensions={0} | all-to-all | bytes 65536 | tf_op jit(solution)/shard_map/all_to_all | solution.py:171
  52.0 29.9 %all_to_all.22 = f32[16,8,256]{2,1,0:T(8,128)S(1)} all-to-all(f32[16,8,256]{2,1,0:T(8,128)S(1)} %broadcast_in_dim.14), channel_id=1, replica_groups=mesh['zl'=4,'y'=8,'c'=2,'zh'=4,'x'=4] {'zh','x'}, dimensions={0} | all-to-all | bytes 262144 | tf_op jit(solution)/shard_map/all_to_all | solution.py:173
  82.0 0.1 broadcast_in_dim.30
  82.1 16.6 %all_to_all.23 = bf16[32,64,128]{2,1,0:T(8,128)(2,1)S(1)} all-to-all(bf16[32,64,128]{2,1,0:T(8,128)(2,1)S(1)} %broadcast_in_dim.30), channel_id=1, replica_groups=mesh['zl'=4,'y'=8,'c'=2,'zh'=4,'x'=4] {'zl','y'}, dimensions={0} | all-to-all | bytes 1048576 | tf_op jit(solution)/shard_map/all_to_all | solution.py:177
  98.7 7.7 %collective-permute-start.1 = (bf16[32,64,128]{2,1,0:T(8,128)(2,1)S(1)}, bf16[32,64,128]{2,1,0:T(8,128)(2,1)S(1)}, u32[]{:S(2)}, u32[]{:S(2)}) collective-permute-start(bf16[32,64,128]{2,1,0:T(8,128)(2,1)S(1)} %all_to_all.23), channel_id=1, source_target_pairs={{0,16},{16,0},{1,17},{17,1},{2,18},{18,2},{3,19},{19,3},{4,20},{20... | collective-permute-start | bytes 1572872 | tf_op jit(solution)/shard_map/ppermute | solution.py:178
  106.4 0.6 divide_subtract_fusion
  107.0 0.8 collective-permute-done.1
  107.9 1.1 %broadcast_select_fusion = bf16[32,2,64,128]{3,2,1,0:T(8,128)(2,1)} fusion(pred[2]{0:T(512)(128)(4,1)S(1)} %iota_compare_fusion, bf16[32,64,128]{2,1,0:T(8,128)(2,1)S(1)} %collective-permute-done.1, bf16[32,64,128]{2,1,0:T(8,128)(2,1)S(1)} %all_to_all.23), kind=kLoop, calls=%fused_computation.4 | loop fusion | flops 524288 | bytes 2097154 | tf_op jit(solution)/shard_map/jit(_where)/select_n | solution.py:180
  (9 shorter events, 0.1 us)
Async XLA Ops:
  0.6 22.0 %copy-start = (f32[8192]{0:T(1024)S(1)}, f32[8192]{0:T(1024)}, u32[]{:S(2)}) copy-start(f32[8192]{0:T(1024)} %param.13) | copy-start | bytes 98308
  0.6 22.0 %copy-start.1 = (f32[8192]{0:T(1024)S(1)}, f32[8192]{0:T(1024)}, u32[]{:S(2)}) copy-start(f32[8192]{0:T(1024)} %param.12) | copy-start | bytes 98308
  6.6 16.1 %copy-start.2 = (f32[8192]{0:T(1024)S(1)}, f32[8192]{0:T(1024)}, u32[]{:S(2)}) copy-start(f32[8192]{0:T(1024)} %param.11) | copy-start | bytes 98308
  6.6 18.3 %collective-permute-start = (f32[32,32,256]{2,1,0:T(8,128)S(1)}, f32[32,32,256]{2,1,0:T(8,128)S(1)}, u32[]{:S(2)}, u32[]{:S(2)}) collective-permute-start(f32[32,32,256]{2,1,0:T(8,128)S(1)} %get-tuple-element.8), channel_id=1, source_target_pairs={{0,16},{16,0},{1,17},{17,1},{2,18},{18,2},{3,19},{19,3},{4,20},{20... | collective-permute-start | bytes 3145736 | tf_op jit(solution)/shard_map/ppermute | solution.py:168
  98.7 9.2 %collective-permute-start.1 = (bf16[32,64,128]{2,1,0:T(8,128)(2,1)S(1)}, bf16[32,64,128]{2,1,0:T(8,128)(2,1)S(1)}, u32[]{:S(2)}, u32[]{:S(2)}) collective-permute-start(bf16[32,64,128]{2,1,0:T(8,128)(2,1)S(1)} %all_to_all.23), channel_id=1, source_target_pairs={{0,16},{16,0},{1,17},{17,1},{2,18},{18,2},{3,19},{19,3},{4,20},{20... | collective-permute-start | bytes 1572872 | tf_op jit(solution)/shard_map/ppermute | solution.py:178

commit v4 on v3

--- a/solution.py
+++ b/solution.py
@@ -104,21 +104,18 @@
             left, right = second_ref[...], cot_ref[...]
         grad = lax.dot_general(left, right, (((0,), (0,)), ((), ())), preferred_element_type=jnp.float32)
         for j in range(0, CH // BLOCK, 2):
+            low = grad[j * BLOCK : (j + 1) * BLOCK, :]
+            high = grad[(j + 1) * BLOCK : (j + 2) * BLOCK, :]
             slot = (k * (CH // BLOCK) + j) // 2
-            for q in range(4):
-                row = j * BLOCK + q * QUARTER
-                low = grad[row : row + QUARTER, :]
-                high = grad[row + BLOCK : row + BLOCK + QUARTER, :]
-                place = (slot % 8) * 4 + q, pl.ds(slot // 8 * QUARTER, QUARTER)
-                keep_ref[place] = jnp.where(even, low, high)
-                send_ref[place] = jnp.where(even, high, low)
+            keep_ref[slot] = jnp.where(even, low, high)
+            send_ref[slot] = jnp.where(even, high, low)
 
 
 def clip_grads(clip, cot, alphas, weights, core):
     frames = clip.shape[0]
     rows = (TAPS + 1) * CH
     vmem = pl.BlockSpec(memory_space=pltpu.VMEM)
-    half = jax.ShapeDtypeStruct((32, 4 * QUARTER, CH), jnp.float32)
+    half = jax.ShapeDtypeStruct((32, BLOCK, CH), jnp.float32)
     return pl.pallas_call(
         unit_kernel,
         out_shape=(half, half),
@@ -166,9 +163,8 @@
     keep, send = clip_grads(clips[0], cotangent[0], alphas, weights, core.reshape(1))
     ready = jnp.concatenate([master, 0.9 * first_moment, 0.999 * second_moment])
     recv, ready = lax.optimization_barrier((lax.ppermute(send, "c", SWAP), ready))
-    part = lax.all_to_all(packed(keep + recv), ("y", "x"), 0, 0, tiled=True)
-    part = jnp.sum(unpacked(part), axis=0).reshape(4, QUARTER, CH)
-    part = jnp.sum(lax.all_to_all(part, "zl", 0, 0, tiled=True), axis=0)
+    part = packed(keep + recv).reshape(128, QUARTER, CH)
+    part = jnp.sum(unpacked(lax.all_to_all(part, ("zl", "y", "x"), 0, 0, tiled=True)), axis=0)
     part = jnp.broadcast_to(part[None], (16, QUARTER, CH))
     part = lax.all_to_all(part, ("zh", "x"), 0, 0, tiled=True)
     gradient = jnp.sum(part.reshape(4, BLOCK, CH), axis=0).reshape(-1)

time: 109 us -> 106 us (0.972)
  blocking collectives: 73 us -> 70.3 us
    all_to_all x2 -> x1, blocking collectives: 26.5 us -> 24.5 us  [shards(): lax.all_to_all(part, ('zl', 'y', 'x'), 0, 0, tiled=True)]
where the time goes in v4:
time: 106 us
  blocking collectives  70.3 us (66%)
  starting transfers between devices  23.3 us (22%)
  Pallas kernels  5.89 us (6%)
  waiting for transfers between devices  3.02 us (3%)
  other arithmetic  2.49 us (2%)
    all_to_all x1, blocking collectives, shards(): part = lax.all_to_all(part, ('zh', 'x'), 0, 0, tiled=True)  28.9 us
    all_to_all x1, blocking collectives, shards(): lax.all_to_all(part, ('zl', 'y', 'x'), 0, 0, tiled=True)  24.5 us
    all_to_all x1, blocking collectives, shards(): lax.all_to_all(jnp.broadcast_to(piece[None], (32, 64, 128)), ('zl', 'y'),...  16.9 us
    ppermute x1, starting transfers between devices, shards(): lax.ppermute(send, 'c', SWAP)  16 us
    ppermute x1, starting transfers between devices, shards(): other = lax.ppermute(piece, 'c', SWAP)  7.31 us
    pallas_call x1, Pallas kernels, clip_grads(): pl.pallas_call(unit_kernel, out_shape=(half, half), in_specs=[pl.BlockSpe...  5.89 us
    ppermute x1, waiting for transfers between devices, shards(): lax.ppermute(send, 'c', SWAP)  2.2 us
  transfers between devices with their start and end apart: 2, of which 2 were waited for; matrix products, arithmetic and copies ran while one was open for 1% of the time, Pallas kernels for 0%

profile of v4, /device:TPU:1, one launch (start us, length us, event | category | flops | bytes accessed | tf_op | source)
XLA Modules:
  0.0 105.9 jit_solution(8677770182607951528)
XLA Ops:
  0.6 0.0 copy-start
  0.6 0.0 copy-start.1
  0.7 5.9 %shard_map.102 = (f32[32,32,256]{2,1,0:T(8,128)S(1)}, f32[32,32,256]{2,1,0:T(8,128)S(1)}) custom-call(s32[1]{0:T(128)} %bitcast.core_ref, bf16[1024,256]{1,0:T(8,128)(2,1)} %bitcast.33, bf16[1024,256]{1,0:T(8,128)(2,1)} %bitcast.34, f32[2,256]{1,0:T(2,128)} %al_hbm.1, bf16[4096,128]{1,0:T(8,128)(2,1)} %bitcast.32), custom_call_target="tpu_custom_call" | custom-call | flops 2200000000 | bytes 5242880 | tf_op jit(solution)/shard_map/pallas_call | solution.py:119
  6.6 0.0 copy-start.2
  6.6 16.0 %collective-permute-start = (f32[32,32,256]{2,1,0:T(8,128)S(1)}, f32[32,32,256]{2,1,0:T(8,128)S(1)}, u32[]{:S(2)}, u32[]{:S(2)}) collective-permute-start(f32[32,32,256]{2,1,0:T(8,128)S(1)} %get-tuple-element.8), channel_id=1, source_target_pairs={{0,16},{16,0},{1,17},{17,1},{2,18},{18,2},{3,19},{19,3},{4,20},{20... | collective-permute-start | bytes 3145736 | tf_op jit(solution)/shard_map/ppermute | solution.py:165
  22.6 0.0 copy-done
  22.6 0.0 copy-done.1
  22.6 0.0 copy-done.2
  22.7 2.2 %collective-permute-done = f32[32,32,256]{2,1,0:T(8,128)S(1)} collective-permute-done((f32[32,32,256]{2,1,0:T(8,128)S(1)}, f32[32,32,256]{2,1,0:T(8,128)S(1)}, u32[]{:S(2)}, u32[]{:S(2)}) %collective-permute-start) | collective-permute-done | bytes 1048608 | tf_op jit(solution)/shard_map/ppermute | solution.py:165
  24.9 0.5 fusion
  25.3 24.5 %all_to_all.15 = f16[128,8,256]{2,1,0:T(8,128)(2,1)S(1)} all-to-all(f16[128,8,256]{2,1,0:T(8,128)(2,1)S(1)} %bitcast.27), channel_id=1, replica_groups=mesh['zl'=4,'y'=8,'c'=2,'zh'=4,'x'=4] {'zl','y','x'}, dimensions={0} | all-to-all | bytes 1048576 | tf_op jit(solution)/shard_map/all_to_all | solution.py:167
  49.8 0.2 fusion.1
  50.0 28.9 %all_to_all.16 = f32[16,8,256]{2,1,0:T(8,128)S(1)} all-to-all(f32[16,8,256]{2,1,0:T(8,128)S(1)} %broadcast_in_dim.14), channel_id=1, replica_groups=mesh['zl'=4,'y'=8,'c'=2,'zh'=4,'x'=4] {'zh','x'}, dimensions={0} | all-to-all | bytes 262144 | tf_op jit(solution)/shard_map/all_to_all | solution.py:169
  79.0 0.1 broadcast_in_dim.30
  79.1 16.9 %all_to_all.17 = bf16[32,64,128]{2,1,0:T(8,128)(2,1)S(1)} all-to-all(bf16[32,64,128]{2,1,0:T(8,128)(2,1)S(1)} %broadcast_in_dim.30), channel_id=1, replica_groups=mesh['zl'=4,'y'=8,'c'=2,'zh'=4,'x'=4] {'zl','y'}, dimensions={0} | all-to-all | bytes 1048576 | tf_op jit(solution)/shard_map/all_to_all | solution.py:173
  96.0 7.3 %collective-permute-start.1 = (bf16[32,64,128]{2,1,0:T(8,128)(2,1)S(1)}, bf16[32,64,128]{2,1,0:T(8,128)(2,1)S(1)}, u32[]{:S(2)}, u32[]{:S(2)}) collective-permute-start(bf16[32,64,128]{2,1,0:T(8,128)(2,1)S(1)} %all_to_all.17), channel_id=1, source_target_pairs={{0,16},{16,0},{1,17},{17,1},{2,18},{18,2},{3,19},{19,3},{4,20},{20... | collective-permute-start | bytes 1572872 | tf_op jit(solution)/shard_map/ppermute | solution.py:174
  103.3 0.6 divide_subtract_fusion
  104.0 0.8 collective-permute-done.1
  104.8 1.1 %broadcast_select_fusion = bf16[32,2,64,128]{3,2,1,0:T(8,128)(2,1)} fusion(pred[2]{0:T(512)(128)(4,1)S(1)} %iota_compare_fusion, bf16[32,64,128]{2,1,0:T(8,128)(2,1)S(1)} %collective-permute-done.1, bf16[32,64,128]{2,1,0:T(8,128)(2,1)S(1)} %all_to_all.17), kind=kLoop, calls=%fused_computation.4 | loop fusion | flops 524288 | bytes 2097154 | tf_op jit(solution)/shard_map/jit(_where)/select_n | solution.py:176
  (8 shorter events, 0.1 us)
Async XLA Ops:
  0.6 22.0 %copy-start = (f32[8192]{0:T(1024)S(1)}, f32[8192]{0:T(1024)}, u32[]{:S(2)}) copy-start(f32[8192]{0:T(1024)} %param.13) | copy-start | bytes 98308
  0.6 22.0 %copy-start.1 = (f32[8192]{0:T(1024)S(1)}, f32[8192]{0:T(1024)}, u32[]{:S(2)}) copy-start(f32[8192]{0:T(1024)} %param.12) | copy-start | bytes 98308
  6.6 16.1 %copy-start.2 = (f32[8192]{0:T(1024)S(1)}, f32[8192]{0:T(1024)}, u32[]{:S(2)}) copy-start(f32[8192]{0:T(1024)} %param.11) | copy-start | bytes 98308
  6.6 18.3 %collective-permute-start = (f32[32,32,256]{2,1,0:T(8,128)S(1)}, f32[32,32,256]{2,1,0:T(8,128)S(1)}, u32[]{:S(2)}, u32[]{:S(2)}) collective-permute-start(f32[32,32,256]{2,1,0:T(8,128)S(1)} %get-tuple-element.8), channel_id=1, source_target_pairs={{0,16},{16,0},{1,17},{17,1},{2,18},{18,2},{3,19},{19,3},{4,20},{20... | collective-permute-start | bytes 3145736 | tf_op jit(solution)/shard_map/ppermute | solution.py:165
  96.0 8.8 %collective-permute-start.1 = (bf16[32,64,128]{2,1,0:T(8,128)(2,1)S(1)}, bf16[32,64,128]{2,1,0:T(8,128)(2,1)S(1)}, u32[]{:S(2)}, u32[]{:S(2)}) collective-permute-start(bf16[32,64,128]{2,1,0:T(8,128)(2,1)S(1)} %all_to_all.17), channel_id=1, source_target_pairs={{0,16},{16,0},{1,17},{17,1},{2,18},{18,2},{3,19},{19,3},{4,20},{20... | collective-permute-start | bytes 1572872 | tf_op jit(solution)/shard_map/ppermute | solution.py:174

commit v5 on v4

--- a/solution.py
+++ b/solution.py
@@ -17,35 +17,29 @@
 BIAS_TWO = 0.09520785288629041
 
 INV_PI = 0.3183098861837907
-PI_A = 3.140625
-PI_B = 9.67502593994140625e-4
-PI_C = 1.509957990978376e-7
 
 
-def reduced(t):
-    n = jnp.round(t * INV_PI)
-    return ((t - n * PI_A) - n * PI_B) - n * PI_C
+def turned(halves):
+    return halves - jnp.round(halves)
 
 
-def sine(r):
-    z = r * r
-    p = -2.4078282e-08
-    for c in (2.75363800e-06, -1.98410853e-04, 8.33333284e-03, -1.66666672e-01):
+def sine(u, z):
+    p = 0.07764279097318649
+    for c in (-0.5982846617698669, 2.550076723098755, -5.167709827423096, 3.1415927410125732):
         p = p * z + c
-    return r + r * (z * p)
+    return u * p
 
 
-def cosine(r):
-    z = r * r
-    p = -2.62950522e-07
-    for c in (2.47744738e-05, -1.38886506e-03, 4.16666605e-02, -0.5):
+def double_cosine(z):
+    p = -0.04924729838967323
+    for c in (0.47014570236206055, -2.6704795360565186, 8.117423057556152, -9.869604110717773, 2.0):
         p = p * z + c
-    return 1.0 + z * p
+    return p
 
 
 def unit_kernel(
     core_ref, x_hbm, cot_hbm, al_hbm, w_hbm, keep_ref, send_ref,
-    x_ref, cot_ref, al_ref, flat_ref, wide_ref, w_ref, pad_ref, first_ref, second_ref, sems,
+    x_ref, cot_ref, al_ref, flat_ref, wide_ref, w_ref, pad_ref, first_ref, second_ref, windows_ref, sems,
 ):
     copies = [
         pltpu.make_async_copy(source, target, sems.at[n])
@@ -58,20 +52,23 @@
     frames = x_ref.shape[0]
     rows = w_ref.shape[0]
     even = core_ref[0] == 0
-    pad_ref[0:PAD, :] = jnp.zeros((PAD, CH), jnp.float32)
-    pad_ref[PAD + frames : 2 * PAD + frames, :] = jnp.zeros((PAD, CH), jnp.float32)
+    pad_ref[0:PAD, :] = jnp.zeros((PAD, CH), jnp.bfloat16)
+    pad_ref[PAD + frames : 2 * PAD + frames, :] = jnp.zeros((PAD, CH), jnp.bfloat16)
     copies[0].wait()
     a0 = al_ref[0:1, :]
     a1 = al_ref[1:2, :]
     r0 = 1.0 / a0
     r1 = 1.0 / a1
+    t0 = a0 * INV_PI
+    t1 = a1 * INV_PI
     copies[1].wait()
     for i in range(0, frames, CHUNK):
         x = x_ref[i : i + CHUNK, :].astype(jnp.float32)
-        s = sine(reduced(a0 * x))
+        u = turned(t0 * x)
+        s = sine(u, u * u)
         first = (x + s * s * r0).astype(jnp.bfloat16)
         first_ref[i : i + CHUNK, :] = first
-        pad_ref[PAD + i : PAD + i + CHUNK, :] = first.astype(jnp.float32)
+        pad_ref[PAD + i : PAD + i + CHUNK, :] = first
     copies[2].wait()
     wide_ref[...] = flat_ref[...].astype(jnp.float32)
     for side in range(2):
@@ -79,27 +76,26 @@
         w_ref[:, side * 128 : (side + 1) * 128] = half.astype(jnp.bfloat16)
     w_point = w_ref[TAPS * CH :, :]
     copies[3].wait()
+    for k in range(TAPS):
+        off = PAD + DILATION * (k - TAPS // 2)
+        windows_ref[:, k * CH : (k + 1) * CH] = pad_ref[off : off + frames, :]
     d_hidden = []
     for i in range(0, frames, CHUNK):
-        hidden = None
-        for k in range(TAPS):
-            off = PAD + i + DILATION * (k - TAPS // 2)
-            window = pad_ref[off : off + CHUNK, :].astype(jnp.bfloat16)
-            part = jnp.dot(window, w_ref[k * CH : (k + 1) * CH, :], preferred_element_type=jnp.float32)
-            hidden = part if hidden is None else hidden + part
-        r = reduced(a1 * hidden)
-        s = sine(r)
+        hidden = jnp.dot(windows_ref[i : i + CHUNK, :], w_ref[: TAPS * CH, :], preferred_element_type=jnp.float32)
+        u = turned(t1 * hidden)
+        z = u * u
+        s = sine(u, z)
         second_ref[i : i + CHUNK, :] = (hidden + s * s * r1).astype(jnp.bfloat16)
         back = lax.dot_general(
             cot_ref[i : i + CHUNK, :], w_point, (((1,), (1,)), ((), ())), preferred_element_type=jnp.float32
         )
-        d_hidden.append((back * (1.0 + 2.0 * s * cosine(r))).astype(jnp.bfloat16).astype(jnp.float32))
+        d_hidden.append((back * (1.0 + s * double_cosine(z))).astype(jnp.bfloat16))
     for n, i in enumerate(range(0, frames, CHUNK)):
         pad_ref[PAD + i : PAD + i + CHUNK, :] = d_hidden[n]
     for k in range(TAPS + 1):
         if k < TAPS:
             off = PAD - DILATION * (k - TAPS // 2)
-            left, right = first_ref[...], pad_ref[off : off + frames, :].astype(jnp.bfloat16)
+            left, right = first_ref[...], pad_ref[off : off + frames, :]
         else:
             left, right = second_ref[...], cot_ref[...]
         grad = lax.dot_general(left, right, (((0,), (0,)), ((), ())), preferred_element_type=jnp.float32)
@@ -128,9 +124,10 @@
             pltpu.VMEM((2 * rows, 128), jnp.bfloat16),
             pltpu.VMEM((2 * rows, 128), jnp.float32),
             pltpu.VMEM((rows, CH), jnp.bfloat16),
-            pltpu.VMEM((frames + 2 * PAD, CH), jnp.float32),
+            pltpu.VMEM((frames + 2 * PAD, CH), jnp.bfloat16),
             pltpu.VMEM((frames, CH), jnp.bfloat16),
             pltpu.VMEM((frames, CH), jnp.bfloat16),
+            pltpu.VMEM((frames, TAPS * CH), jnp.bfloat16),
             pltpu.SemaphoreType.DMA((4,)),
         ],
         compiler_params=pltpu.CompilerParams(vmem_limit_bytes=40 << 20),

time: 106 us -> 106 us (level)
  no operation moved by 1% of the time
where the time goes in v5:
time: 106 us; the launch traced here: 105 us
  blocking collectives  70.2 us (66%)
  starting transfers between devices  23.3 us (22%)
  Pallas kernels  5.26 us (5%)
  waiting for transfers between devices  3.02 us (3%)
  other arithmetic  2.49 us (2%)
    all_to_all x1, blocking collectives, shards(): part = lax.all_to_all(part, ('zh', 'x'), 0, 0, tiled=True)  28.9 us
    all_to_all x1, blocking collectives, shards(): lax.all_to_all(part, ('zl', 'y', 'x'), 0, 0, tiled=True)  24.5 us
    all_to_all x1, blocking collectives, shards(): lax.all_to_all(jnp.broadcast_to(piece[None], (32, 64, 128)), ('zl', 'y'),...  16.9 us
    ppermute x1, starting transfers between devices, shards(): lax.ppermute(send, 'c', SWAP)  16 us
    ppermute x1, starting transfers between devices, shards(): other = lax.ppermute(piece, 'c', SWAP)  7.31 us
    pallas_call x1, Pallas kernels, clip_grads(): pl.pallas_call(unit_kernel, out_shape=(half, half), in_specs=[pl.BlockSpe...  5.26 us
    ppermute x1, waiting for transfers between devices, shards(): lax.ppermute(send, 'c', SWAP)  2.2 us
  transfers between devices with their start and end apart: 2, of which 2 were waited for; matrix products, arithmetic and copies ran while one was open for 1% of the time, Pallas kernels for 0%

profile of v5, /device:TPU:1, one launch (start us, length us, event | category | flops | bytes accessed | tf_op | source)
XLA Modules:
  0.0 105.3 jit_solution(13437732021946206508)
XLA Ops:
  0.6 0.0 copy-start
  0.6 0.0 copy-start.1
  0.7 5.3 %shard_map.102 = (f32[32,32,256]{2,1,0:T(8,128)S(1)}, f32[32,32,256]{2,1,0:T(8,128)S(1)}) custom-call(s32[1]{0:T(128)} %bitcast.core_ref, bf16[1024,256]{1,0:T(8,128)(2,1)} %bitcast.33, bf16[1024,256]{1,0:T(8,128)(2,1)} %bitcast.34, f32[2,256]{1,0:T(2,128)} %al_hbm.1, bf16[4096,128]{1,0:T(8,128)(2,1)} %bitcast.32), custom_call_target="tpu_custom_call" | custom-call | flops 2200000000 | bytes 5242880 | tf_op jit(solution)/shard_map/pallas_call | solution.py:115
  5.9 0.0 copy-start.2
  5.9 16.0 %collective-permute-start = (f32[32,32,256]{2,1,0:T(8,128)S(1)}, f32[32,32,256]{2,1,0:T(8,128)S(1)}, u32[]{:S(2)}, u32[]{:S(2)}) collective-permute-start(f32[32,32,256]{2,1,0:T(8,128)S(1)} %get-tuple-element.8), channel_id=1, source_target_pairs={{0,16},{16,0},{1,17},{17,1},{2,18},{18,2},{3,19},{19,3},{4,20},{20... | collective-permute-start | bytes 3145736 | tf_op jit(solution)/shard_map/ppermute | solution.py:162
  22.0 0.0 copy-done
  22.0 0.0 copy-done.1
  22.0 0.0 copy-done.2
  22.0 2.2 %collective-permute-done = f32[32,32,256]{2,1,0:T(8,128)S(1)} collective-permute-done((f32[32,32,256]{2,1,0:T(8,128)S(1)}, f32[32,32,256]{2,1,0:T(8,128)S(1)}, u32[]{:S(2)}, u32[]{:S(2)}) %collective-permute-start) | collective-permute-done | bytes 1048608 | tf_op jit(solution)/shard_map/ppermute | solution.py:162
  24.2 0.5 fusion
  24.7 24.5 %all_to_all.15 = f16[128,8,256]{2,1,0:T(8,128)(2,1)S(1)} all-to-all(f16[128,8,256]{2,1,0:T(8,128)(2,1)S(1)} %bitcast.27), channel_id=1, replica_groups=mesh['zl'=4,'y'=8,'c'=2,'zh'=4,'x'=4] {'zl','y','x'}, dimensions={0} | all-to-all | bytes 1048576 | tf_op jit(solution)/shard_map/all_to_all | solution.py:164
  49.2 0.2 fusion.1
  49.4 28.9 %all_to_all.16 = f32[16,8,256]{2,1,0:T(8,128)S(1)} all-to-all(f32[16,8,256]{2,1,0:T(8,128)S(1)} %broadcast_in_dim.14), channel_id=1, replica_groups=mesh['zl'=4,'y'=8,'c'=2,'zh'=4,'x'=4] {'zh','x'}, dimensions={0} | all-to-all | bytes 262144 | tf_op jit(solution)/shard_map/all_to_all | solution.py:166
  78.4 0.1 broadcast_in_dim.30
  78.5 16.9 %all_to_all.17 = bf16[32,64,128]{2,1,0:T(8,128)(2,1)S(1)} all-to-all(bf16[32,64,128]{2,1,0:T(8,128)(2,1)S(1)} %broadcast_in_dim.30), channel_id=1, replica_groups=mesh['zl'=4,'y'=8,'c'=2,'zh'=4,'x'=4] {'zl','y'}, dimensions={0} | all-to-all | bytes 1048576 | tf_op jit(solution)/shard_map/all_to_all | solution.py:170
  95.3 7.3 %collective-permute-start.1 = (bf16[32,64,128]{2,1,0:T(8,128)(2,1)S(1)}, bf16[32,64,128]{2,1,0:T(8,128)(2,1)S(1)}, u32[]{:S(2)}, u32[]{:S(2)}) collective-permute-start(bf16[32,64,128]{2,1,0:T(8,128)(2,1)S(1)} %all_to_all.17), channel_id=1, source_target_pairs={{0,16},{16,0},{1,17},{17,1},{2,18},{18,2},{3,19},{19,3},{4,20},{20... | collective-permute-start | bytes 1572872 | tf_op jit(solution)/shard_map/ppermute | solution.py:171
  102.7 0.6 divide_subtract_fusion
  103.3 0.8 collective-permute-done.1
  104.2 1.1 %broadcast_select_fusion = bf16[32,2,64,128]{3,2,1,0:T(8,128)(2,1)} fusion(pred[2]{0:T(512)(128)(4,1)S(1)} %iota_compare_fusion, bf16[32,64,128]{2,1,0:T(8,128)(2,1)S(1)} %collective-permute-done.1, bf16[32,64,128]{2,1,0:T(8,128)(2,1)S(1)} %all_to_all.17), kind=kLoop, calls=%fused_computation.4 | loop fusion | flops 524288 | bytes 2097154 | tf_op jit(solution)/shard_map/jit(_where)/select_n | solution.py:173
  (8 shorter events, 0.1 us)
Async XLA Ops:
  0.6 21.3 %copy-start = (f32[8192]{0:T(1024)S(1)}, f32[8192]{0:T(1024)}, u32[]{:S(2)}) copy-start(f32[8192]{0:T(1024)} %param.13) | copy-start | bytes 98308
  0.6 21.3 %copy-start.1 = (f32[8192]{0:T(1024)S(1)}, f32[8192]{0:T(1024)}, u32[]{:S(2)}) copy-start(f32[8192]{0:T(1024)} %param.12) | copy-start | bytes 98308
  5.9 16.1 %copy-start.2 = (f32[8192]{0:T(1024)S(1)}, f32[8192]{0:T(1024)}, u32[]{:S(2)}) copy-start(f32[8192]{0:T(1024)} %param.11) | copy-start | bytes 98308
  5.9 18.3 %collective-permute-start = (f32[32,32,256]{2,1,0:T(8,128)S(1)}, f32[32,32,256]{2,1,0:T(8,128)S(1)}, u32[]{:S(2)}, u32[]{:S(2)}) collective-permute-start(f32[32,32,256]{2,1,0:T(8,128)S(1)} %get-tuple-element.8), channel_id=1, source_target_pairs={{0,16},{16,0},{1,17},{17,1},{2,18},{18,2},{3,19},{19,3},{4,20},{20... | collective-permute-start | bytes 3145736 | tf_op jit(solution)/shard_map/ppermute | solution.py:162
  95.3 8.8 %collective-permute-start.1 = (bf16[32,64,128]{2,1,0:T(8,128)(2,1)S(1)}, bf16[32,64,128]{2,1,0:T(8,128)(2,1)S(1)}, u32[]{:S(2)}, u32[]{:S(2)}) collective-permute-start(bf16[32,64,128]{2,1,0:T(8,128)(2,1)S(1)} %all_to_all.17), channel_id=1, source_target_pairs={{0,16},{16,0},{1,17},{17,1},{2,18},{18,2},{3,19},{19,3},{4,20},{20... | collective-permute-start | bytes 1572872 | tf_op jit(solution)/shard_map/ppermute | solution.py:171

commit v6 on v5

--- a/solution.py
+++ b/solution.py
@@ -41,15 +41,13 @@
     core_ref, x_hbm, cot_hbm, al_hbm, w_hbm, keep_ref, send_ref,
     x_ref, cot_ref, al_ref, flat_ref, wide_ref, w_ref, pad_ref, first_ref, second_ref, windows_ref, sems,
 ):
-    copies = [
-        pltpu.make_async_copy(source, target, sems.at[n])
-        for n, (source, target) in enumerate(
-            ((al_hbm, al_ref), (x_hbm, x_ref), (w_hbm, flat_ref), (cot_hbm, cot_ref))
-        )
-    ]
+    frames = x_ref.shape[0]
+    pairs = [(al_hbm, al_ref), (w_hbm, flat_ref), (cot_hbm, cot_ref)]
+    for i in range(0, frames, CHUNK):
+        pairs.insert(1 + i // CHUNK, (x_hbm.at[pl.ds(i, CHUNK)], x_ref.at[pl.ds(i, CHUNK)]))
+    copies = [pltpu.make_async_copy(source, target, sems.at[n]) for n, (source, target) in enumerate(pairs)]
     for copy in copies:
         copy.start()
-    frames = x_ref.shape[0]
     rows = w_ref.shape[0]
     even = core_ref[0] == 0
     pad_ref[0:PAD, :] = jnp.zeros((PAD, CH), jnp.bfloat16)
@@ -61,21 +59,21 @@
     r1 = 1.0 / a1
     t0 = a0 * INV_PI
     t1 = a1 * INV_PI
-    copies[1].wait()
     for i in range(0, frames, CHUNK):
+        copies[1 + i // CHUNK].wait()
         x = x_ref[i : i + CHUNK, :].astype(jnp.float32)
         u = turned(t0 * x)
         s = sine(u, u * u)
         first = (x + s * s * r0).astype(jnp.bfloat16)
         first_ref[i : i + CHUNK, :] = first
         pad_ref[PAD + i : PAD + i + CHUNK, :] = first
-    copies[2].wait()
+    copies[-2].wait()
     wide_ref[...] = flat_ref[...].astype(jnp.float32)
     for side in range(2):
         half = wide_ref[pl.ds(side, rows, stride=2), :]
         w_ref[:, side * 128 : (side + 1) * 128] = half.astype(jnp.bfloat16)
     w_point = w_ref[TAPS * CH :, :]
-    copies[3].wait()
+    copies[-1].wait()
     for k in range(TAPS):
         off = PAD + DILATION * (k - TAPS // 2)
         windows_ref[:, k * CH : (k + 1) * CH] = pad_ref[off : off + frames, :]
@@ -128,11 +126,37 @@
             pltpu.VMEM((frames, CH), jnp.bfloat16),
             pltpu.VMEM((frames, CH), jnp.bfloat16),
             pltpu.VMEM((frames, TAPS * CH), jnp.bfloat16),
-            pltpu.SemaphoreType.DMA((4,)),
+            pltpu.SemaphoreType.DMA((3 + frames // CHUNK,)),
         ],
         compiler_params=pltpu.CompilerParams(vmem_limit_bytes=40 << 20),
         cost_estimate=pl.CostEstimate(flops=2200000000, bytes_accessed=5 << 20, transcendentals=0),
     )(core, *[pltpu.with_memory_space_constraint(v, pltpu.HBM) for v in (clip, cot, alphas, weights.reshape(2 * rows, 128))])
+
+
+def first_half_kernel(core_ref, piece_ref, out_ref, sem):
+    copy = pltpu.make_async_copy(piece_ref, out_ref.at[:, core_ref[0]], sem)
+    copy.start()
+    copy.wait()
+
+
+def second_half_kernel(core_ref, piece_ref, begun_ref, out_ref, sem):
+    copy = pltpu.make_async_copy(piece_ref, out_ref.at[:, 1 - core_ref[0]], sem)
+    copy.start()
+    copy.wait()
+
+
+def place(kernel, core, piece, *begun):
+    hbm = pl.BlockSpec(memory_space=pltpu.HBM)
+    return pl.pallas_call(
+        kernel,
+        out_shape=jax.ShapeDtypeStruct((32, 2, 64, 128), jnp.bfloat16),
+        in_specs=[pl.BlockSpec(memory_space=pltpu.SMEM), pl.BlockSpec(memory_space=pltpu.VMEM)] + [hbm] * len(begun),
+        out_specs=hbm,
+        scratch_shapes=[pltpu.SemaphoreType.DMA],
+        input_output_aliases={2: 0} if begun else {},
+        compiler_params=pltpu.CompilerParams(vmem_limit_bytes=4 << 20),
+        cost_estimate=pl.CostEstimate(flops=0, bytes_accessed=1 << 20, transcendentals=0),
+    )(core, piece, *begun)
 
 
 def adam_update(gradient, master, first_part, second_part):
@@ -146,8 +170,7 @@
 
 
 def packed(values):
-    root = jnp.sqrt(jnp.abs(values))
-    return jnp.where(values < 0, -root, root).astype(jnp.float16)
+    return (values * lax.rsqrt(jnp.maximum(jnp.abs(values), 1e-30))).astype(jnp.float16)
 
 
 def unpacked(roots):
@@ -156,8 +179,8 @@
 
 
 def shards(clips, cotangent, alphas, weights, master, first_moment, second_moment):
-    core = lax.axis_index("c")
-    keep, send = clip_grads(clips[0], cotangent[0], alphas, weights, core.reshape(1))
+    core = lax.axis_index("c").reshape(1)
+    keep, send = clip_grads(clips[0], cotangent[0], alphas, weights, core)
     ready = jnp.concatenate([master, 0.9 * first_moment, 0.999 * second_moment])
     recv, ready = lax.optimization_barrier((lax.ppermute(send, "c", SWAP), ready))
     part = packed(keep + recv).reshape(128, QUARTER, CH)
@@ -169,8 +192,8 @@
     piece = new_master.astype(jnp.bfloat16).reshape(64, 128)
     piece = lax.all_to_all(jnp.broadcast_to(piece[None], (32, 64, 128)), ("zl", "y"), 0, 0, tiled=True)
     other = lax.ppermute(piece, "c", SWAP)
-    place = lax.broadcasted_iota(jnp.int32, (32, 2, 64, 128), 1)
-    new_weights = jnp.where(place == core, piece[:, None], other[:, None]).reshape(-1)
+    half = place(first_half_kernel, core, piece)
+    new_weights = place(second_half_kernel, core, other, half).reshape(-1)
     return (new_weights, new_master, new_first, new_second)
 
 

time: 106 us -> 105 us (level)
  Pallas kernels: 5.26 us -> 6.78 us
  other arithmetic: 2.49 us -> 1.17 us
    pallas_call x0 -> x2, Pallas kernels: none -> 1.6 us  [place(): pl.pallas_call(kernel, out_shape=jax.ShapeDtypeStruct((32, 2, 64, 128), j...]
    select_n x1 -> x0, other arithmetic: 1.11 us -> none  [shards(): jnp.where(place == core, piece[:, None], other[:, None]).reshape(-1)]
  transfers between devices with their start and end apart: 2 -> 2, of which waited for: 2 -> 1; matrix products, arithmetic and copies ran while one was open for 1% -> 1% of each run, Pallas kernels for 0% -> 1%
where the time goes in v6:
time: 105 us
  blocking collectives  70.3 us (67%)
  starting transfers between devices  23.3 us (22%)
  Pallas kernels  6.78 us (6%)
  waiting for transfers between devices  2.23 us (2%)
  other arithmetic  1.17 us (1%)
    all_to_all x1, blocking collectives, shards(): part = lax.all_to_all(part, ('zh', 'x'), 0, 0, tiled=True)  28.9 us
    all_to_all x1, blocking collectives, shards(): lax.all_to_all(part, ('zl', 'y', 'x'), 0, 0, tiled=True)  24.5 us
    all_to_all x1, blocking collectives, shards(): lax.all_to_all(jnp.broadcast_to(piece[None], (32, 64, 128)), ('zl', 'y'),...  16.9 us
    ppermute x1, starting transfers between devices, shards(): lax.ppermute(send, 'c', SWAP)  16 us
    ppermute x1, starting transfers between devices, shards(): other = lax.ppermute(piece, 'c', SWAP)  7.31 us
    pallas_call x1, Pallas kernels, clip_grads(): pl.pallas_call(unit_kernel, out_shape=(half, half), in_specs=[pl.BlockSpe...  5.18 us
    ppermute x1, waiting for transfers between devices, shards(): lax.ppermute(send, 'c', SWAP)  2.2 us
  transfers between devices with their start and end apart: 2, of which 1 were waited for; matrix products, arithmetic and copies ran while one was open for 1% of the time, Pallas kernels for 1%

profile of v6, /device:TPU:1, one launch (start us, length us, event | category | flops | bytes accessed | tf_op | source)
XLA Modules:
  0.0 104.7 jit_solution(11048418134191397523)
XLA Ops:
  0.6 0.0 copy-start
  0.6 0.0 copy-start.1
  0.7 5.2 %shard_map.102 = (f32[32,32,256]{2,1,0:T(8,128)S(1)}, f32[32,32,256]{2,1,0:T(8,128)S(1)}) custom-call(s32[1]{0:T(128)} %bitcast.core_ref, bf16[1024,256]{1,0:T(8,128)(2,1)} %bitcast.33, bf16[1024,256]{1,0:T(8,128)(2,1)} %bitcast.34, f32[2,256]{1,0:T(2,128)} %al_hbm.1, bf16[4096,128]{1,0:T(8,128)(2,1)} %bitcast.32), custom_call_target="tpu_custom_call" | custom-call | flops 2200000000 | bytes 5242880 | tf_op jit(solution)/shard_map/pallas_call | solution.py:113
  5.8 0.0 copy-start.2
  5.9 16.0 %collective-permute-start = (f32[32,32,256]{2,1,0:T(8,128)S(1)}, f32[32,32,256]{2,1,0:T(8,128)S(1)}, u32[]{:S(2)}, u32[]{:S(2)}) collective-permute-start(f32[32,32,256]{2,1,0:T(8,128)S(1)} %get-tuple-element.8), channel_id=1, source_target_pairs={{0,16},{16,0},{1,17},{17,1},{2,18},{18,2},{3,19},{19,3},{4,20},{20... | collective-permute-start | bytes 3145736 | tf_op jit(solution)/shard_map/ppermute | solution.py:185
  21.9 0.0 copy-done
  21.9 0.0 copy-done.1
  21.9 0.0 copy-done.2
  21.9 2.2 %collective-permute-done = f32[32,32,256]{2,1,0:T(8,128)S(1)} collective-permute-done((f32[32,32,256]{2,1,0:T(8,128)S(1)}, f32[32,32,256]{2,1,0:T(8,128)S(1)}, u32[]{:S(2)}, u32[]{:S(2)}) %collective-permute-start) | collective-permute-done | bytes 1048608 | tf_op jit(solution)/shard_map/ppermute | solution.py:185
  24.1 0.3 multiply_convert_fusion
  24.4 24.5 %all_to_all.15 = f16[128,8,256]{2,1,0:T(8,128)(2,1)S(1)} all-to-all(f16[128,8,256]{2,1,0:T(8,128)(2,1)S(1)} %bitcast.28), channel_id=1, replica_groups=mesh['zl'=4,'y'=8,'c'=2,'zh'=4,'x'=4] {'zl','y','x'}, dimensions={0} | all-to-all | bytes 1048576 | tf_op jit(solution)/shard_map/all_to_all | solution.py:187
  48.9 0.2 fusion
  49.1 28.9 %all_to_all.16 = f32[16,8,256]{2,1,0:T(8,128)S(1)} all-to-all(f32[16,8,256]{2,1,0:T(8,128)S(1)} %broadcast_in_dim.4), channel_id=1, replica_groups=mesh['zl'=4,'y'=8,'c'=2,'zh'=4,'x'=4] {'zh','x'}, dimensions={0} | all-to-all | bytes 262144 | tf_op jit(solution)/shard_map/all_to_all | solution.py:189
  78.1 0.1 broadcast_in_dim.5
  78.2 16.9 %all_to_all.17.piece_ref = bf16[32,64,128]{2,1,0:T(8,128)(2,1)S(1)} all-to-all(bf16[32,64,128]{2,1,0:T(8,128)(2,1)S(1)} %broadcast_in_dim.5), channel_id=1, replica_groups=mesh['zl'=4,'y'=8,'c'=2,'zh'=4,'x'=4] {'zl','y'}, dimensions={0} | all-to-all | bytes 1048576 | tf_op jit(solution)/shard_map/all_to_all | solution.py:193
  95.1 7.3 %collective-permute-start.1 = (bf16[32,64,128]{2,1,0:T(8,128)(2,1)S(1)}, bf16[32,64,128]{2,1,0:T(8,128)(2,1)S(1)}, u32[]{:S(2)}, u32[]{:S(2)}) collective-permute-start(bf16[32,64,128]{2,1,0:T(8,128)(2,1)S(1)} %all_to_all.17.piece_ref), channel_id=1, source_target_pairs={{0,16},{16,0},{1,17},{17,1},{2,18},{18,2},{3,19},{19,3},{4,20},{20... | collective-permute-start | bytes 1572872 | tf_op jit(solution)/shard_map/ppermute | solution.py:194
  102.4 0.6 divide_subtract_fusion
  103.1 0.8 shard_map.103.begun_ref
  103.9 0.0 collective-permute-done.1.piece_ref
  103.9 0.8 shard_map.104
  (7 shorter events, 0.1 us)
Async XLA Ops:
  0.6 21.2 %copy-start = (f32[8192]{0:T(1024)S(1)}, f32[8192]{0:T(1024)}, u32[]{:S(2)}) copy-start(f32[8192]{0:T(1024)} %param.13) | copy-start | bytes 98308
  0.6 21.2 %copy-start.1 = (f32[8192]{0:T(1024)S(1)}, f32[8192]{0:T(1024)}, u32[]{:S(2)}) copy-start(f32[8192]{0:T(1024)} %param.12) | copy-start | bytes 98308
  5.8 16.1 %copy-start.2 = (f32[8192]{0:T(1024)S(1)}, f32[8192]{0:T(1024)}, u32[]{:S(2)}) copy-start(f32[8192]{0:T(1024)} %param.11) | copy-start | bytes 98308
  5.9 18.3 %collective-permute-start = (f32[32,32,256]{2,1,0:T(8,128)S(1)}, f32[32,32,256]{2,1,0:T(8,128)S(1)}, u32[]{:S(2)}, u32[]{:S(2)}) collective-permute-start(f32[32,32,256]{2,1,0:T(8,128)S(1)} %get-tuple-element.8), channel_id=1, source_target_pairs={{0,16},{16,0},{1,17},{17,1},{2,18},{18,2},{3,19},{19,3},{4,20},{20... | collective-permute-start | bytes 3145736 | tf_op jit(solution)/shard_map/ppermute | solution.py:185
  95.1 8.8 %collective-permute-start.1 = (bf16[32,64,128]{2,1,0:T(8,128)(2,1)S(1)}, bf16[32,64,128]{2,1,0:T(8,128)(2,1)S(1)}, u32[]{:S(2)}, u32[]{:S(2)}) collective-permute-start(bf16[32,64,128]{2,1,0:T(8,128)(2,1)S(1)} %all_to_all.17.piece_ref), channel_id=1, source_target_pairs={{0,16},{16,0},{1,17},{17,1},{2,18},{18,2},{3,19},{19,3},{4,20},{20... | collective-permute-start | bytes 1572872 | tf_op jit(solution)/shard_map/ppermute | solution.py:194

commit v7 on v6

--- a/solution.py
+++ b/solution.py
@@ -11,7 +11,6 @@
 PAD = 16
 CHUNK = 256
 BLOCK = 32
-QUARTER = BLOCK // 4
 
 BIAS_ONE = 0.9999734386011124
 BIAS_TWO = 0.09520785288629041
@@ -183,11 +182,12 @@
     keep, send = clip_grads(clips[0], cotangent[0], alphas, weights, core)
     ready = jnp.concatenate([master, 0.9 * first_moment, 0.999 * second_moment])
     recv, ready = lax.optimization_barrier((lax.ppermute(send, "c", SWAP), ready))
-    part = packed(keep + recv).reshape(128, QUARTER, CH)
-    part = jnp.sum(unpacked(lax.all_to_all(part, ("zl", "y", "x"), 0, 0, tiled=True)), axis=0)
-    part = jnp.broadcast_to(part[None], (16, QUARTER, CH))
-    part = lax.all_to_all(part, ("zh", "x"), 0, 0, tiled=True)
-    gradient = jnp.sum(part.reshape(4, BLOCK, CH), axis=0).reshape(-1)
+    part = lax.all_to_all(packed(keep + recv), ("zl", "y"), 0, 0, tiled=True)
+    part = jnp.sum(unpacked(part), axis=0)
+    for axis in ("x", "zh"):
+        part = jnp.broadcast_to(part[None], (4, BLOCK, CH))
+        part = jnp.sum(lax.all_to_all(part, axis, 0, 0, tiled=True), axis=0)
+    gradient = part.reshape(-1)
     new_master, new_first, new_second = adam_update(gradient, *jnp.split(ready, 3))
     piece = new_master.astype(jnp.bfloat16).reshape(64, 128)
     piece = lax.all_to_all(jnp.broadcast_to(piece[None], (32, 64, 128)), ("zl", "y"), 0, 0, tiled=True)

time: 105 us -> 106 us (level)
  blocking collectives: 70.3 us -> 71.4 us
    all_to_all x1, blocking collectives: 16.9 us -> 19.9 us  [shards(): lax.all_to_all(jnp.broadcast_to(piece[None], (32, 64, 128)), ('zl', 'y'),...]
    all_to_all x2 -> x3, blocking collectives: 53.4 us -> 51.6 us  [the longest x2 33 us: shards(): part = jnp.sum(lax.all_to_all(part, axis, 0, 0, tiled=True), axis=0)]
where the time goes in v7:
time: 106 us
  blocking collectives  71.4 us (67%)
  starting transfers between devices  23.1 us (22%)
  Pallas kernels  6.78 us (6%)
  waiting for transfers between devices  2.23 us (2%)
  other arithmetic  1.14 us (1%)
    all_to_all x2, blocking collectives, shards(): part = jnp.sum(lax.all_to_all(part, axis, 0, 0, tiled=True), axis=0)  33 us
    all_to_all x1, blocking collectives, shards(): lax.all_to_all(jnp.broadcast_to(piece[None], (32, 64, 128)), ('zl', 'y'),...  19.9 us
    all_to_all x1, blocking collectives, shards(): part = lax.all_to_all(packed(keep + recv), ('zl', 'y'), 0, 0, tiled=True)  18.6 us
    ppermute x1, starting transfers between devices, shards(): lax.ppermute(send, 'c', SWAP)  16 us
    ppermute x1, starting transfers between devices, shards(): other = lax.ppermute(piece, 'c', SWAP)  7.11 us
    pallas_call x1, Pallas kernels, clip_grads(): pl.pallas_call(unit_kernel, out_shape=(half, half), in_specs=[pl.BlockSpe...  5.18 us
    ppermute x1, waiting for transfers between devices, shards(): lax.ppermute(send, 'c', SWAP)  2.2 us
  transfers between devices with their start and end apart: 2, of which 1 were waited for; matrix products, arithmetic and copies ran while one was open for 1% of the time, Pallas kernels for 1%

profile of v7, /device:TPU:1, one launch (start us, length us, event | category | flops | bytes accessed | tf_op | source)
XLA Modules:
  0.0 105.7 jit_solution(2766028089665794491)
XLA Ops:
  0.6 0.0 copy-start
  0.6 0.0 copy-start.1
  0.7 5.2 %shard_map.102 = (f32[32,32,256]{2,1,0:T(8,128)S(1)}, f32[32,32,256]{2,1,0:T(8,128)S(1)}) custom-call(s32[1]{0:T(128)} %bitcast.core_ref, bf16[1024,256]{1,0:T(8,128)(2,1)} %bitcast.27, bf16[1024,256]{1,0:T(8,128)(2,1)} %bitcast.28, f32[2,256]{1,0:T(2,128)} %al_hbm.1, bf16[4096,128]{1,0:T(8,128)(2,1)} %bitcast.26), custom_call_target="tpu_custom_call" | custom-call | flops 2200000000 | bytes 5242880 | tf_op jit(solution)/shard_map/pallas_call | solution.py:112
  5.8 0.0 copy-start.2
  5.9 16.0 %collective-permute-start = (f32[32,32,256]{2,1,0:T(8,128)S(1)}, f32[32,32,256]{2,1,0:T(8,128)S(1)}, u32[]{:S(2)}, u32[]{:S(2)}) collective-permute-start(f32[32,32,256]{2,1,0:T(8,128)S(1)} %get-tuple-element.8), channel_id=1, source_target_pairs={{0,16},{16,0},{1,17},{17,1},{2,18},{18,2},{3,19},{19,3},{4,20},{20... | collective-permute-start | bytes 3145736 | tf_op jit(solution)/shard_map/ppermute | solution.py:184
  21.9 0.0 copy-done
  21.9 0.0 copy-done.1
  21.9 0.0 copy-done.2
  21.9 2.2 %collective-permute-done = f32[32,32,256]{2,1,0:T(8,128)S(1)} collective-permute-done((f32[32,32,256]{2,1,0:T(8,128)S(1)}, f32[32,32,256]{2,1,0:T(8,128)S(1)}, u32[]{:S(2)}, u32[]{:S(2)}) %collective-permute-start) | collective-permute-done | bytes 1048608 | tf_op jit(solution)/shard_map/ppermute | solution.py:184
  24.1 0.3 multiply_convert_fusion
  24.4 18.6 %all_to_all.20 = f16[32,32,256]{2,1,0:T(8,128)(2,1)S(1)} all-to-all(f16[32,32,256]{2,1,0:T(8,128)(2,1)S(1)} %multiply_convert_fusion), channel_id=1, replica_groups=mesh['zl'=4,'y'=8,'c'=2,'zh'=4,'x'=4] {'zl','y'}, dimensions={0} | all-to-all | bytes 1048576 | tf_op jit(solution)/shard_map/all_to_all | solution.py:185
  43.0 0.1 fusion
  43.2 7.2 %all_to_all.21 = f32[4,32,256]{2,1,0:T(8,128)S(1)} all-to-all(f32[4,32,256]{2,1,0:T(8,128)S(1)} %broadcast_in_dim.6), channel_id=1, replica_groups=mesh['zl'=4,'y'=8,'c'=2,'zh'=4,'x'=4] {'x'}, dimensions={0} | all-to-all | bytes 262144 | tf_op jit(solution)/shard_map/all_to_all | solution.py:189
  50.4 25.8 %all_to_all.22 = f32[4,32,256]{2,1,0:T(8,128)S(1)} all-to-all(f32[4,32,256]{2,1,0:T(8,128)S(1)} %broadcast_in_dim.7), channel_id=1, replica_groups=mesh['zl'=4,'y'=8,'c'=2,'zh'=4,'x'=4] {'zh'}, dimensions={0} | all-to-all | bytes 262144 | tf_op jit(solution)/shard_map/all_to_all | solution.py:189
  76.3 0.1 broadcast_in_dim.8
  76.4 19.9 %all_to_all.23.piece_ref = bf16[32,64,128]{2,1,0:T(8,128)(2,1)S(1)} all-to-all(bf16[32,64,128]{2,1,0:T(8,128)(2,1)S(1)} %broadcast_in_dim.8), channel_id=1, replica_groups=mesh['zl'=4,'y'=8,'c'=2,'zh'=4,'x'=4] {'zl','y'}, dimensions={0} | all-to-all | bytes 1048576 | tf_op jit(solution)/shard_map/all_to_all | solution.py:193
  96.2 7.1 %collective-permute-start.1 = (bf16[32,64,128]{2,1,0:T(8,128)(2,1)S(1)}, bf16[32,64,128]{2,1,0:T(8,128)(2,1)S(1)}, u32[]{:S(2)}, u32[]{:S(2)}) collective-permute-start(bf16[32,64,128]{2,1,0:T(8,128)(2,1)S(1)} %all_to_all.23.piece_ref), channel_id=1, source_target_pairs={{0,16},{16,0},{1,17},{17,1},{2,18},{18,2},{3,19},{19,3},{4,20},{20... | collective-permute-start | bytes 1572872 | tf_op jit(solution)/shard_map/ppermute | solution.py:194
  103.4 0.6 divide_subtract_fusion
  104.0 0.8 shard_map.103.begun_ref
  104.8 0.0 collective-permute-done.1.piece_ref
  104.9 0.8 shard_map.104
  (9 shorter events, 0.1 us)
Async XLA Ops:
  0.6 21.2 %copy-start = (f32[8192]{0:T(1024)S(1)}, f32[8192]{0:T(1024)}, u32[]{:S(2)}) copy-start(f32[8192]{0:T(1024)} %param.13) | copy-start | bytes 98308
  0.6 21.2 %copy-start.1 = (f32[8192]{0:T(1024)S(1)}, f32[8192]{0:T(1024)}, u32[]{:S(2)}) copy-start(f32[8192]{0:T(1024)} %param.12) | copy-start | bytes 98308
  5.8 16.1 %copy-start.2 = (f32[8192]{0:T(1024)S(1)}, f32[8192]{0:T(1024)}, u32[]{:S(2)}) copy-start(f32[8192]{0:T(1024)} %param.11) | copy-start | bytes 98308
  5.9 18.3 %collective-permute-start = (f32[32,32,256]{2,1,0:T(8,128)S(1)}, f32[32,32,256]{2,1,0:T(8,128)S(1)}, u32[]{:S(2)}, u32[]{:S(2)}) collective-permute-start(f32[32,32,256]{2,1,0:T(8,128)S(1)} %get-tuple-element.8), channel_id=1, source_target_pairs={{0,16},{16,0},{1,17},{17,1},{2,18},{18,2},{3,19},{19,3},{4,20},{20... | collective-permute-start | bytes 3145736 | tf_op jit(solution)/shard_map/ppermute | solution.py:184
  96.2 8.6 %collective-permute-start.1 = (bf16[32,64,128]{2,1,0:T(8,128)(2,1)S(1)}, bf16[32,64,128]{2,1,0:T(8,128)(2,1)S(1)}, u32[]{:S(2)}, u32[]{:S(2)}) collective-permute-start(bf16[32,64,128]{2,1,0:T(8,128)(2,1)S(1)} %all_to_all.23.piece_ref), channel_id=1, source_target_pairs={{0,16},{16,0},{1,17},{17,1},{2,18},{18,2},{3,19},{19,3},{4,20},{20... | collective-permute-start | bytes 1572872 | tf_op jit(solution)/shard_map/ppermute | solution.py:194
